TPU v7x, 512 devices: a whole 4x4x16 slice. The times are simulated.
512 devices in a mesh: blk: 32 (over y_lo, z), gy: 4 (over x), rep: 4 (over y_hi, core).
Axes of the slice: x: 4, y: 4 (y_hi: 2, y_lo: 2; y = y_hi * 2 + y_lo), z: 16, core: 2. Of those that a mesh axis runs over, the one named last changes fastest.
Arguments:
- grain_id: int32 [128, 32, 512], P('blk', 'gy', 'rep'), may hold values from 0 to 255
- init_masks: int32 [2, 128, 32, 512], P(None, 'blk', 'gy', 'rep'), may hold values from 0 to 1, as said below
- target_masks: int32 [2, 128, 32, 512], P(None, 'blk', 'gy', 'rep'), may hold values from 0 to 1, as said below
- emb_table: bfloat16 [256, 8], replicated, may hold values from -6 to 6
- w_in: float32 [64, 10], P('rep'), may hold values from -2 to 2
- b_in: float32 [64], P('rep'), may hold values from -3 to 3
- w_mid: float32 [64, 64], P('rep'), may hold values from -0.75 to 0.75
- b_mid: float32 [64], P('rep'), may hold values from -3 to 3
- w_out: float32 [6, 64], P(None, 'rep'), may hold values from -0.75 to 0.75
- b_out: float32 [6], replicated, may hold values from -4 to 4
Outputs:
- final_state: float32 [2, 128, 32, 512], P(None, 'blk', 'gy', 'rep')
- loss: float32 [], replicated
- grad_w_in: float32 [64, 10], P('rep')
- grad_b_in: float32 [64], P('rep')
- grad_w_mid: float32 [64, 64], P('rep')
- grad_b_mid: float32 [64], P('rep')
- grad_w_out: float32 [6, 64], P(None, 'rep')
- grad_b_out: float32 [6], replicated
- start_sensitivity: float32 [2, 128, 32, 512], P(None, 'blk', 'gy', 'rep')
Inputs may be any that keep to these rules, and one draw needn't show every extreme that they name: `init_masks`: 0 or 1 in every cell. `target_masks`: 0 or 1 in every cell.
All inputs are finite; a program needn't handle non-finite values.
Results may differ from a plain program's by a relative error of at most 0.0054.
The roundings to bfloat16 on the way count: a program that leaves them out, or rounds other values in their place, can miss the bound.
Values may be sent and summed in bfloat16 or wider, within the bound.
A program may use at most 64 MiB of HBM per device.

v0:
```python
import jax
import jax.numpy as jnp
from jax import lax
from jax.sharding import PartitionSpec as P

STEPS = 4
RATE_MAX = 0.15


def extended(block, sides, width):
    for axis, dim in sides:
        count = lax.axis_size(axis)
        forward = [(i, i + 1) for i in range(count - 1)]
        forward.append((count - 1, 0))
        backward = [(target, source) for source, target in forward]
        low = lax.ppermute(
            lax.slice_in_dim(block, block.shape[dim] - width, None, axis=dim), axis, forward
        )
        high = lax.ppermute(lax.slice_in_dim(block, 0, width, axis=dim), axis, backward)
        block = jnp.concatenate([low, block, high], axis=dim)
    return block


def beside(padded, axis_pos, offset):
    index_list = [slice(None), slice(1, -1), slice(1, -1), slice(1, -1)]
    index_list[axis_pos] = slice(1 + offset, padded.shape[axis_pos] - 1 + offset)
    return padded[tuple(index_list)]


def interior(padded):
    return padded[:, 1:-1, 1:-1, 1:-1]


def diffuse(field_pad, rate_pad):
    centre = interior(field_pad)
    summed = centre
    rate_centre = interior(rate_pad)
    for direction in range(3):
        axis_pos = 3 - direction
        rate_here = rate_centre[direction::3]
        for offset in (1, -1):
            rate_next = beside(rate_pad, axis_pos, offset)[direction::3]
            summed = summed + 0.5 * (rate_here + rate_next) * (
                beside(field_pad, axis_pos, offset) - centre
            )
    return summed


def rate_cotangent(state_pad, adjoint_pad):
    centre_state = interior(state_pad)
    centre_adjoint = interior(adjoint_pad)
    pieces_list = []
    for direction in range(3):
        axis_pos = 3 - direction
        summed = jnp.zeros_like(centre_state)
        for offset in (1, -1):
            summed = summed + (beside(state_pad, axis_pos, offset) - centre_state) * (
                beside(adjoint_pad, axis_pos, offset) - centre_adjoint
            )
        pieces_list.append(-0.5 * summed)
    stacked = jnp.stack(pieces_list, axis=1)
    return stacked.reshape((6,) + stacked.shape[2:])


def embed_lookup(emb_table, grain_flat):
    table_rows = emb_table.shape[0]
    one_hot = (grain_flat[None, :] == lax.broadcasted_iota(jnp.int32, (table_rows, 1), 0)).astype(
        jnp.bfloat16
    )
    looked = jnp.dot(emb_table.T, one_hot, preferred_element_type=jnp.float32)
    return looked.astype(jnp.bfloat16)


def forward_layers(params, features):
    w_in, b_in, w_mid, b_mid, w_out, b_out = params
    act_one = jnp.tanh(
        jnp.dot(w_in, features, preferred_element_type=jnp.float32)
        + b_in.astype(jnp.float32)[:, None]
    )
    hid_one = act_one.astype(jnp.bfloat16)
    act_two = jnp.tanh(
        jnp.dot(w_mid, hid_one, preferred_element_type=jnp.float32)
        + b_mid.astype(jnp.float32)[:, None]
    )
    hid_two = act_two.astype(jnp.bfloat16)
    logits = (
        jnp.dot(w_out, hid_two, preferred_element_type=jnp.float32)
        + b_out.astype(jnp.float32)[:, None]
    )
    return (RATE_MAX * jax.nn.sigmoid(logits), act_one, hid_one, act_two, hid_two)


def backward_layers(params, features, rate_grad, forward_values):
    w_in, b_in, w_mid, b_mid, w_out, b_out = params
    rate_values, act_one, hid_one, act_two, hid_two = forward_values
    out_grad = (rate_grad * rate_values * (1.0 - rate_values / RATE_MAX)).astype(jnp.bfloat16)
    two_grad = (
        jnp.dot(w_out.T, out_grad, preferred_element_type=jnp.float32) * (1.0 - act_two * act_two)
    ).astype(jnp.bfloat16)
    one_grad = (
        jnp.dot(w_mid.T, two_grad, preferred_element_type=jnp.float32) * (1.0 - act_one * act_one)
    ).astype(jnp.bfloat16)
    grad_terms = (
        jnp.dot(one_grad, features.T, preferred_element_type=jnp.float32),
        jnp.sum(one_grad, axis=1, dtype=jnp.float32),
        jnp.dot(two_grad, hid_one.T, preferred_element_type=jnp.float32),
        jnp.sum(two_grad, axis=1, dtype=jnp.float32),
        jnp.dot(out_grad, hid_two.T, preferred_element_type=jnp.float32),
        jnp.sum(out_grad, axis=1, dtype=jnp.float32),
    )
    state_grad = jnp.dot(w_in[:, -2:].T, one_grad, preferred_element_type=jnp.float32)
    return (grad_terms, state_grad)


def per_device(
    grain_id, init_masks, target_masks, emb_table, w_in, b_in, w_mid, b_mid, w_out, b_out
):
    w_in_b, b_in_b, w_mid_b, b_mid_b, w_out_b = (
        lax.all_gather(w_in.astype(jnp.bfloat16), "rep", axis=0, tiled=True),
        lax.all_gather(b_in.astype(jnp.bfloat16), "rep", axis=0, tiled=True),
        lax.all_gather(w_mid.astype(jnp.bfloat16), "rep", axis=0, tiled=True),
        lax.all_gather(b_mid.astype(jnp.bfloat16), "rep", axis=0, tiled=True),
        lax.all_gather(w_out.astype(jnp.bfloat16), "rep", axis=1, tiled=True),
    )
    params = (w_in_b, b_in_b, w_mid_b, b_mid_b, w_out_b, b_out.astype(jnp.bfloat16))
    depth_cells, row_cells, col_cells = grain_id.shape
    cell_count = depth_cells * row_cells * col_cells
    embedding = embed_lookup(emb_table, grain_id.reshape(cell_count))
    state_now = init_masks.astype(jnp.float32)
    history = []
    for step_index in range(STEPS):
        features = jnp.concatenate(
            [embedding, state_now.reshape(2, cell_count).astype(jnp.bfloat16)], axis=0
        )
        rate_values = forward_layers(params, features)[0].reshape(
            6, depth_cells, row_cells, col_cells
        )
        joined = extended(
            jnp.concatenate([state_now, rate_values], axis=0),
            (("blk", 1), ("gy", 2), ("rep", 3)),
            1,
        )
        state_pad = joined[:2]
        rate_pad = joined[2:]
        history.append((state_pad, rate_pad))
        state_now = diffuse(state_pad, rate_pad)
    misfit = state_now - target_masks.astype(jnp.float32)
    total_cells = float(
        cell_count * lax.axis_size("blk") * lax.axis_size("gy") * lax.axis_size("rep")
    )
    loss_part = jnp.sum(misfit * misfit) / (4.0 * total_cells)
    adjoint = misfit / (2.0 * total_cells)
    grad_sums = None
    for step_index in reversed(range(STEPS)):
        state_pad, rate_pad = history[step_index]
        adjoint_pad = extended(adjoint, (("blk", 1), ("gy", 2), ("rep", 3)), 1)
        rate_grad = rate_cotangent(state_pad, adjoint_pad).reshape(6, cell_count)
        features = jnp.concatenate(
            [embedding, interior(state_pad).reshape(2, cell_count).astype(jnp.bfloat16)], axis=0
        )
        forward_values = forward_layers(params, features)
        step_terms, state_grad = backward_layers(params, features, rate_grad, forward_values)
        if grad_sums is None:
            grad_sums = step_terms
        else:
            grad_sums = tuple(
                (earlier + later_term for earlier, later_term in zip(grad_sums, step_terms))
            )
        adjoint = diffuse(adjoint_pad, rate_pad) + state_grad.reshape(
            2, depth_cells, row_cells, col_cells
        )
    start_sensitivity = adjoint * (2.0 * total_cells)
    sum_w_in, sum_b_in, sum_w_mid, sum_b_mid, sum_w_out, sum_b_out = grad_sums
    summed = lax.psum(
        (sum_w_in, sum_b_in, sum_w_mid, sum_b_mid, sum_w_out, sum_b_out, loss_part),
        ("blk", "gy", "rep"),
    )
    position = lax.axis_index("rep")
    share_width = w_in.shape[0]
    grad_w_in = lax.dynamic_slice_in_dim(summed[0], position * share_width, share_width, 0)
    grad_b_in = lax.dynamic_slice_in_dim(summed[1], position * share_width, share_width, 0)
    grad_w_mid = lax.dynamic_slice_in_dim(summed[2], position * share_width, share_width, 0)
    grad_b_mid = lax.dynamic_slice_in_dim(summed[3], position * share_width, share_width, 0)
    grad_w_out = lax.dynamic_slice_in_dim(summed[4], position * share_width, share_width, 1)
    grad_b_out = summed[5]
    loss_total = summed[6]
    return (
        state_now,
        loss_total,
        grad_w_in,
        grad_b_in,
        grad_w_mid,
        grad_b_mid,
        grad_w_out,
        grad_b_out,
        start_sensitivity,
    )


def solution(mesh):
    in_specs = (
        P("blk", "gy", "rep"),
        P(None, "blk", "gy", "rep"),
        P(None, "blk", "gy", "rep"),
        P(),
        P("rep", None),
        P("rep"),
        P("rep", None),
        P("rep"),
        P(None, "rep"),
        P(),
    )
    out_specs = (
        P(None, "blk", "gy", "rep"),
        P(),
        P("rep", None),
        P("rep"),
        P("rep", None),
        P("rep"),
        P(None, "rep"),
        P(),
        P(None, "blk", "gy", "rep"),
    )
    return jax.shard_map(
        per_device, mesh=mesh, in_specs=in_specs, out_specs=out_specs, check_vma=False
    )
```

profile of v0, /device:TPU:1, one launch (start us, length us, event | category | flops | bytes accessed | tf_op | source)
XLA Modules:
  0.0 452.5 jit_solution(13899464881031292997)
XLA Ops:
  5.0 13.4 %all-reduce.3 = (bf16[64]{0:T(256)(128)(2,1)S(1)}, bf16[64]{0:T(256)(128)(2,1)S(1)}) all-reduce(bf16[64]{0:T(256)(128)(2,1)S(1)} %dynamic-update-slice.1, bf16[64]{0:T(256)(128)(2,1)S(1)} %dynamic-update-slice), channel_id=1, replica_groups=mesh['blk'=32,'gy'=4,'rep'=4] {'rep'}, use_global_device_ids=true, to_apply=%add.1 | all-reduce | flops 128 | bytes 512
  20.5 7.2 %all-gather = bf16[4,16,6]{1,2,0:T(8,128)(2,1)S(1)} all-gather(bf16[1,16,6]{1,2,0:T(8,128)(2,1)S(1)} %convert_bitcast_fusion.4), channel_id=1, replica_groups=mesh['blk'=32,'gy'=4,'rep'=4] {'rep'}, dimensions={0}, use_global_device_ids=true | all-gather | bytes 960 | tf_op jit(solution)/shard_map/all_gather | solution.py:123
  27.8 6.7 %all_gather.17 = bf16[64,64]{1,0:T(8,128)(2,1)S(1)} all-gather(bf16[16,64]{1,0:T(8,128)(2,1)S(1)} %convert_element_type.210), channel_id=1, replica_groups=mesh['blk'=32,'gy'=4,'rep'=4] {'rep'}, dimensions={0}, use_global_device_ids=true | all-gather | bytes 10240 | tf_op jit(solution)/shard_map/all_gather | solution.py:121
  34.5 6.7 %all_gather.15 = bf16[64,10]{1,0:T(8,128)(2,1)S(1)} all-gather(bf16[16,10]{1,0:T(8,128)(2,1)S(1)} %convert_element_type.206), channel_id=1, replica_groups=mesh['blk'=32,'gy'=4,'rep'=4] {'rep'}, dimensions={0}, use_global_device_ids=true | all-gather | bytes 1600 | tf_op jit(solution)/shard_map/all_gather | solution.py:119
  44.3 8.7 %collective-permute-start.1 = (f32[8,1,8,128]{3,2,1,0:T(8,128)S(1)}, f32[8,1,8,128]{3,2,1,0:T(8,128)S(1)}, u32[]{:S(2)}, u32[]{:S(2)}) collective-permute-start(f32[8,1,8,128]{3,2,1,0:T(8,128)S(1)} %get-tuple-element.100), channel_id=1, source_target_pairs={{16,0},{32,16},{48,32},{64,48},{80,64},{96,80},{112,96},{128,112},... | collective-permute-start | bytes 98312 | tf_op jit(solution)/shard_map/ppermute | solution.py:19
  54.9 4.8 %collective-permute-done = f32[8,1,8,128]{3,2,1,0:T(8,128)S(1)} collective-permute-done((f32[8,1,8,128]{3,2,1,0:T(8,128)S(1)}, f32[8,1,8,128]{3,2,1,0:T(8,128)S(1)}, u32[]{:S(2)}, u32[]{:S(2)}) %collective-permute-start) | collective-permute-done | bytes 32800 | tf_op jit(solution)/shard_map/ppermute | solution.py:16
  59.8 4.4 collective-permute-start.3
  66.2 3.7 collective-permute-done.2
  70.2 5.0 %collective-permute-start.4 = (f32[8,6,10,1]{3,2,1,0:T(8,128)S(1)}, f32[8,6,10,1]{3,2,1,0:T(8,128)S(1)}, u32[]{:S(2)}, u32[]{:S(2)}) collective-permute-start(f32[8,6,10,1]{3,2,1,0:T(8,128)S(1)} %get-tuple-element.64), channel_id=1, source_target_pairs={{1,0},{2,1},{3,2},{0,3},{5,4},{6,5},{7,6},{4,7},{9,8},{10,9},{11,1... | collective-permute-start | bytes 5768 | tf_op jit(solution)/shard_map/ppermute | solution.py:19
  75.2 3.3 collective-permute-start.5
  78.6 4.9 %collective-permute-done.4 = f32[8,6,10,1]{3,2,1,0:T(8,128)S(1)} collective-permute-done((f32[8,6,10,1]{3,2,1,0:T(8,128)S(1)}, f32[8,6,10,1]{3,2,1,0:T(8,128)S(1)}, u32[]{:S(2)}, u32[]{:S(2)}) %collective-permute-start.4) | collective-permute-done | bytes 1952 | tf_op jit(solution)/shard_map/ppermute | solution.py:19
  89.2 3.4 collective-permute-start.6
  92.6 3.4 collective-permute-done.6
  97.9 3.4 collective-permute-start.8
  104.0 6.9 %collective-permute-start.10 = (f32[8,6,10,1]{3,2,1,0:T(8,128)S(1)}, f32[8,6,10,1]{3,2,1,0:T(8,128)S(1)}, u32[]{:S(2)}, u32[]{:S(2)}) collective-permute-start(f32[8,6,10,1]{3,2,1,0:T(8,128)S(1)} %get-tuple-element.62), channel_id=1, source_target_pairs={{1,0},{2,1},{3,2},{0,3},{5,4},{6,5},{7,6},{4,7},{9,8},{10,9},{11,1... | collective-permute-start | bytes 5768 | tf_op jit(solution)/shard_map/ppermute | solution.py:19
  110.9 3.5 collective-permute-start.11
  114.4 5.1 %collective-permute-done.10 = f32[8,6,10,1]{3,2,1,0:T(8,128)S(1)} collective-permute-done((f32[8,6,10,1]{3,2,1,0:T(8,128)S(1)}, f32[8,6,10,1]{3,2,1,0:T(8,128)S(1)}, u32[]{:S(2)}, u32[]{:S(2)}) %collective-permute-start.10) | collective-permute-done | bytes 1952 | tf_op jit(solution)/shard_map/ppermute | solution.py:19
  124.9 3.4 collective-permute-start.12
  128.2 3.4 collective-permute-done.12
  133.6 3.4 collective-permute-start.14
  139.6 7.1 %collective-permute-start.16 = (f32[8,6,10,1]{3,2,1,0:T(8,128)S(1)}, f32[8,6,10,1]{3,2,1,0:T(8,128)S(1)}, u32[]{:S(2)}, u32[]{:S(2)}) collective-permute-start(f32[8,6,10,1]{3,2,1,0:T(8,128)S(1)} %get-tuple-element.60), channel_id=1, source_target_pairs={{1,0},{2,1},{3,2},{0,3},{5,4},{6,5},{7,6},{4,7},{9,8},{10,9},{11,1... | collective-permute-start | bytes 5768 | tf_op jit(solution)/shard_map/ppermute | solution.py:19
  146.7 3.3 collective-permute-start.17
  150.1 4.9 %collective-permute-done.16 = f32[8,6,10,1]{3,2,1,0:T(8,128)S(1)} collective-permute-done((f32[8,6,10,1]{3,2,1,0:T(8,128)S(1)}, f32[8,6,10,1]{3,2,1,0:T(8,128)S(1)}, u32[]{:S(2)}, u32[]{:S(2)}) %collective-permute-start.16) | collective-permute-done | bytes 1952 | tf_op jit(solution)/shard_map/ppermute | solution.py:19
  160.4 3.4 collective-permute-start.18
  163.8 3.4 collective-permute-done.18
  169.2 3.4 collective-permute-start.20
  175.2 7.1 %collective-permute-start.22 = (f32[8,6,10,1]{3,2,1,0:T(8,128)S(1)}, f32[8,6,10,1]{3,2,1,0:T(8,128)S(1)}, u32[]{:S(2)}, u32[]{:S(2)}) collective-permute-start(f32[8,6,10,1]{3,2,1,0:T(8,128)S(1)} %get-tuple-element.58), channel_id=1, source_target_pairs={{1,0},{2,1},{3,2},{0,3},{5,4},{6,5},{7,6},{4,7},{9,8},{10,9},{11,1... | collective-permute-start | bytes 5768 | tf_op jit(solution)/shard_map/ppermute | solution.py:19
  182.3 3.5 collective-permute-start.23
  185.9 5.1 %collective-permute-done.22 = f32[8,6,10,1]{3,2,1,0:T(8,128)S(1)} collective-permute-done((f32[8,6,10,1]{3,2,1,0:T(8,128)S(1)}, f32[8,6,10,1]{3,2,1,0:T(8,128)S(1)}, u32[]{:S(2)}, u32[]{:S(2)}) %collective-permute-start.22) | collective-permute-done | bytes 1952 | tf_op jit(solution)/shard_map/ppermute | solution.py:19
  195.6 5.5 %collective-permute-start.25 = (f32[2,1,8,128]{3,2,1,0:T(8,128)}, f32[2,1,8,128]{3,2,1,0:T(8,128)}, u32[]{:S(2)}, u32[]{:S(2)}) collective-permute-start(f32[2,1,8,128]{3,2,1,0:T(8,128)} %get-tuple-element.133), channel_id=1, source_target_pairs={{16,0},{32,16},{48,32},{64,48},{80,64},{96,80},{112,96},{128,112},... | collective-permute-start | bytes 24584 | tf_op jit(solution)/shard_map/ppermute | solution.py:19
  205.8 4.2 collective-permute-start.27
  213.0 7.6 %collective-permute-start.29 = (f32[2,6,10,1]{3,2,1,0:T(8,128)S(1)}, f32[2,6,10,1]{3,2,1,0:T(8,128)S(1)}, u32[]{:S(2)}, u32[]{:S(2)}) collective-permute-start(f32[2,6,10,1]{3,2,1,0:T(8,128)S(1)} %get-tuple-element.108), channel_id=1, source_target_pairs={{0,1},{1,2},{2,3},{3,0},{4,5},{5,6},{6,7},{7,4},{8,9},{9,10},{10,1... | collective-permute-start | bytes 1448 | tf_op jit(solution)/shard_map/ppermute | solution.py:16
  223.8 4.2 collective-permute-done.28
  240.4 5.7 %collective-permute-start.31 = (f32[2,1,8,128]{3,2,1,0:T(8,128)S(1)}, f32[2,1,8,128]{3,2,1,0:T(8,128)S(1)}, u32[]{:S(2)}, u32[]{:S(2)}) collective-permute-start(f32[2,1,8,128]{3,2,1,0:T(8,128)S(1)} %get-tuple-element.131), channel_id=1, source_target_pairs={{16,0},{32,16},{48,32},{64,48},{80,64},{96,80},{112,96},{128,112},... | collective-permute-start | bytes 24584 | tf_op jit(solution)/shard_map/ppermute | solution.py:19
  248.8 4.7 %collective-permute-start.33 = (f32[2,6,1,128]{3,2,1,0:T(1,128)S(1)}, f32[2,6,1,128]{3,2,1,0:T(1,128)S(1)}, u32[]{:S(2)}, u32[]{:S(2)}) collective-permute-start(f32[2,6,1,128]{3,2,1,0:T(1,128)S(1)} %get-tuple-element.121), channel_id=1, source_target_pairs={{4,0},{8,4},{12,8},{0,12},{5,1},{9,5},{13,9},{1,13},{6,2},{10,6},{... | collective-permute-start | bytes 18440 | tf_op jit(solution)/shard_map/ppermute | solution.py:19
  254.6 4.1 collective-permute-start.35
  260.7 5.4 %collective-permute-done.34 = f32[2,6,10,1]{3,2,1,0:T(8,128)S(1)} collective-permute-done((f32[2,6,10,1]{3,2,1,0:T(8,128)S(1)}, f32[2,6,10,1]{3,2,1,0:T(8,128)S(1)}, u32[]{:S(2)}, u32[]{:S(2)}) %collective-permute-start.34) | collective-permute-done | bytes 512 | tf_op jit(solution)/shard_map/ppermute | solution.py:19
  278.2 5.6 %collective-permute-start.37 = (f32[2,1,8,128]{3,2,1,0:T(8,128)S(1)}, f32[2,1,8,128]{3,2,1,0:T(8,128)S(1)}, u32[]{:S(2)}, u32[]{:S(2)}) collective-permute-start(f32[2,1,8,128]{3,2,1,0:T(8,128)S(1)} %get-tuple-element.129), channel_id=1, source_target_pairs={{16,0},{32,16},{48,32},{64,48},{80,64},{96,80},{112,96},{128,112},... | collective-permute-start | bytes 24584 | tf_op jit(solution)/shard_map/ppermute | solution.py:19
  284.6 3.2 collective-permute-start.38
  287.7 3.9 collective-permute-start.39
  292.7 4.2 collective-permute-start.41
  298.9 5.4 %collective-permute-done.40 = f32[2,6,10,1]{3,2,1,0:T(8,128)S(1)} collective-permute-done((f32[2,6,10,1]{3,2,1,0:T(8,128)S(1)}, f32[2,6,10,1]{3,2,1,0:T(8,128)S(1)}, u32[]{:S(2)}, u32[]{:S(2)}) %collective-permute-start.40) | collective-permute-done | bytes 512 | tf_op jit(solution)/shard_map/ppermute | solution.py:19
  313.7 5.6 %collective-permute-start.43 = (f32[2,1,8,128]{3,2,1,0:T(8,128)S(1)}, f32[2,1,8,128]{3,2,1,0:T(8,128)S(1)}, u32[]{:S(2)}, u32[]{:S(2)}) collective-permute-start(f32[2,1,8,128]{3,2,1,0:T(8,128)S(1)} %get-tuple-element.127), channel_id=1, source_target_pairs={{16,0},{32,16},{48,32},{64,48},{80,64},{96,80},{112,96},{128,112},... | collective-permute-start | bytes 24584 | tf_op jit(solution)/shard_map/ppermute | solution.py:19
  320.1 3.6 collective-permute-start.44
  323.7 3.1 collective-permute-start.45
  328.2 4.7 %collective-permute-start.47 = (f32[2,6,10,1]{3,2,1,0:T(8,128)S(1)}, f32[2,6,10,1]{3,2,1,0:T(8,128)S(1)}, u32[]{:S(2)}, u32[]{:S(2)}) collective-permute-start(f32[2,6,10,1]{3,2,1,0:T(8,128)S(1)} %get-tuple-element.102), channel_id=1, source_target_pairs={{0,1},{1,2},{2,3},{3,0},{4,5},{5,6},{6,7},{7,4},{8,9},{9,10},{10,1... | collective-permute-start | bytes 1448 | tf_op jit(solution)/shard_map/ppermute | solution.py:16
  334.9 5.4 %collective-permute-done.46 = f32[2,6,10,1]{3,2,1,0:T(8,128)S(1)} collective-permute-done((f32[2,6,10,1]{3,2,1,0:T(8,128)S(1)}, f32[2,6,10,1]{3,2,1,0:T(8,128)S(1)}, u32[]{:S(2)}, u32[]{:S(2)}) %collective-permute-start.46) | collective-permute-done | bytes 512 | tf_op jit(solution)/shard_map/ppermute | solution.py:19
  343.8 104.1 %all-reduce.2 = (f32[]{:T(128)}, f32[64,10]{1,0:T(8,128)S(1)}, f32[64]{0:T(128)S(1)}, f32[64,64]{1,0:T(8,128)S(1)}, f32[64]{0:T(128)S(1)}, /*index=5*/f32[6,64]{1,0:T(8,128)S(1)}, f32[6]{0:T(128)}) all-reduce(f32[]{:T(128)S(6)} %div.30, ...), channel_id=1, replica_groups=mesh['blk'=32,'gy'=4,'rep'=4] {'blk','gy','rep'}, use_global_device_ids=true, to_apply=%region_1.0 | all-reduce | flops 5255 | bytes 42040 | tf_op jit(solution)/shard_map/psum | solution.py:174
  (432 shorter events, 112.5 us)
Async XLA Ops:
  44.3 10.6 %collective-permute-start.1 = (f32[8,1,8,128]{3,2,1,0:T(8,128)S(1)}, f32[8,1,8,128]{3,2,1,0:T(8,128)S(1)}, u32[]{:S(2)}, u32[]{:S(2)}) collective-permute-start(f32[8,1,8,128]{3,2,1,0:T(8,128)S(1)} %get-tuple-element.100), channel_id=1, source_target_pairs={{16,0},{32,16},{48,32},{64,48},{80,64},{96,80},{112,96},{128,112},... | collective-permute-start | bytes 98312 | tf_op jit(solution)/shard_map/ppermute | solution.py:19
  53.0 6.8 %collective-permute-start = (f32[8,1,8,128]{3,2,1,0:T(8,128)S(1)}, f32[8,1,8,128]{3,2,1,0:T(8,128)S(1)}, u32[]{:S(2)}, u32[]{:S(2)}) collective-permute-start(f32[8,1,8,128]{3,2,1,0:T(8,128)S(1)} %get-tuple-element.101), channel_id=1, source_target_pairs={{0,16},{16,32},{32,48},{48,64},{64,80},{80,96},{96,112},{112,128},... | collective-permute-start | bytes 98312 | tf_op jit(solution)/shard_map/ppermute | solution.py:16
  59.8 6.4 %collective-permute-start.3 = (f32[8,6,1,128]{3,2,1,0:T(1,128)S(1)}, f32[8,6,1,128]{3,2,1,0:T(1,128)S(1)}, u32[]{:S(2)}, u32[]{:S(2)}) collective-permute-start(f32[8,6,1,128]{3,2,1,0:T(1,128)S(1)} %get-tuple-element.84), channel_id=1, source_target_pairs={{4,0},{8,4},{12,8},{0,12},{5,1},{9,5},{13,9},{1,13},{6,2},{10,6},{... | collective-permute-start | bytes 73736 | tf_op jit(solution)/shard_map/ppermute | solution.py:19
  64.2 5.8 %collective-permute-start.2 = (f32[8,6,1,128]{3,2,1,0:T(1,128)S(1)}, f32[8,6,1,128]{3,2,1,0:T(1,128)S(1)}, u32[]{:S(2)}, u32[]{:S(2)}) collective-permute-start(f32[8,6,1,128]{3,2,1,0:T(1,128)S(1)} %get-tuple-element.85), channel_id=1, source_target_pairs={{0,4},{4,8},{8,12},{12,0},{1,5},{5,9},{9,13},{13,1},{2,6},{6,10},{... | collective-permute-start | bytes 73736 | tf_op jit(solution)/shard_map/ppermute | solution.py:16
  70.2 13.2 %collective-permute-start.4 = (f32[8,6,10,1]{3,2,1,0:T(8,128)S(1)}, f32[8,6,10,1]{3,2,1,0:T(8,128)S(1)}, u32[]{:S(2)}, u32[]{:S(2)}) collective-permute-start(f32[8,6,10,1]{3,2,1,0:T(8,128)S(1)} %get-tuple-element.64), channel_id=1, source_target_pairs={{1,0},{2,1},{3,2},{0,3},{5,4},{6,5},{7,6},{4,7},{9,8},{10,9},{11,1... | collective-permute-start | bytes 5768 | tf_op jit(solution)/shard_map/ppermute | solution.py:19
  75.2 9.1 %collective-permute-start.5 = (f32[8,6,10,1]{3,2,1,0:T(8,128)S(1)}, f32[8,6,10,1]{3,2,1,0:T(8,128)S(1)}, u32[]{:S(2)}, u32[]{:S(2)}) collective-permute-start(f32[8,6,10,1]{3,2,1,0:T(8,128)S(1)} %get-tuple-element.65), channel_id=1, source_target_pairs={{0,1},{1,2},{2,3},{3,0},{4,5},{5,6},{6,7},{7,4},{8,9},{9,10},{10,1... | collective-permute-start | bytes 5768 | tf_op jit(solution)/shard_map/ppermute | solution.py:16
  87.3 5.3 %collective-permute-start.7 = (f32[8,1,8,128]{3,2,1,0:T(8,128)S(1)}, f32[8,1,8,128]{3,2,1,0:T(8,128)S(1)}, u32[]{:S(2)}, u32[]{:S(2)}) collective-permute-start(f32[8,1,8,128]{3,2,1,0:T(8,128)S(1)} %get-tuple-element.96), channel_id=1, source_target_pairs={{16,0},{32,16},{48,32},{64,48},{80,64},{96,80},{112,96},{128,112},... | collective-permute-start | bytes 98312 | tf_op jit(solution)/shard_map/ppermute | solution.py:19
  89.2 6.8 %collective-permute-start.6 = (f32[8,1,8,128]{3,2,1,0:T(8,128)S(1)}, f32[8,1,8,128]{3,2,1,0:T(8,128)S(1)}, u32[]{:S(2)}, u32[]{:S(2)}) collective-permute-start(f32[8,1,8,128]{3,2,1,0:T(8,128)S(1)} %get-tuple-element.97), channel_id=1, source_target_pairs={{0,16},{16,32},{32,48},{48,64},{64,80},{80,96},{96,112},{112,128},... | collective-permute-start | bytes 98312 | tf_op jit(solution)/shard_map/ppermute | solution.py:16
  96.0 5.4 %collective-permute-start.9 = (f32[8,6,1,128]{3,2,1,0:T(1,128)S(1)}, f32[8,6,1,128]{3,2,1,0:T(1,128)S(1)}, u32[]{:S(2)}, u32[]{:S(2)}) collective-permute-start(f32[8,6,1,128]{3,2,1,0:T(1,128)S(1)} %get-tuple-element.82), channel_id=1, source_target_pairs={{4,0},{8,4},{12,8},{0,12},{5,1},{9,5},{13,9},{1,13},{6,2},{10,6},{... | collective-permute-start | bytes 73736 | tf_op jit(solution)/shard_map/ppermute | solution.py:19
  97.9 5.8 %collective-permute-start.8 = (f32[8,6,1,128]{3,2,1,0:T(1,128)S(1)}, f32[8,6,1,128]{3,2,1,0:T(1,128)S(1)}, u32[]{:S(2)}, u32[]{:S(2)}) collective-permute-start(f32[8,6,1,128]{3,2,1,0:T(1,128)S(1)} %get-tuple-element.83), channel_id=1, source_target_pairs={{0,4},{4,8},{8,12},{12,0},{1,5},{5,9},{9,13},{13,1},{2,6},{6,10},{... | collective-permute-start | bytes 73736 | tf_op jit(solution)/shard_map/ppermute | solution.py:16
  104.0 15.5 %collective-permute-start.10 = (f32[8,6,10,1]{3,2,1,0:T(8,128)S(1)}, f32[8,6,10,1]{3,2,1,0:T(8,128)S(1)}, u32[]{:S(2)}, u32[]{:S(2)}) collective-permute-start(f32[8,6,10,1]{3,2,1,0:T(8,128)S(1)} %get-tuple-element.62), channel_id=1, source_target_pairs={{1,0},{2,1},{3,2},{0,3},{5,4},{6,5},{7,6},{4,7},{9,8},{10,9},{11,1... | collective-permute-start | bytes 5768 | tf_op jit(solution)/shard_map/ppermute | solution.py:19
  110.9 9.1 %collective-permute-start.11 = (f32[8,6,10,1]{3,2,1,0:T(8,128)S(1)}, f32[8,6,10,1]{3,2,1,0:T(8,128)S(1)}, u32[]{:S(2)}, u32[]{:S(2)}) collective-permute-start(f32[8,6,10,1]{3,2,1,0:T(8,128)S(1)} %get-tuple-element.63), channel_id=1, source_target_pairs={{0,1},{1,2},{2,3},{3,0},{4,5},{5,6},{6,7},{7,4},{8,9},{9,10},{10,1... | collective-permute-start | bytes 5768 | tf_op jit(solution)/shard_map/ppermute | solution.py:16
  122.9 5.3 %collective-permute-start.13 = (f32[8,1,8,128]{3,2,1,0:T(8,128)S(1)}, f32[8,1,8,128]{3,2,1,0:T(8,128)S(1)}, u32[]{:S(2)}, u32[]{:S(2)}) collective-permute-start(f32[8,1,8,128]{3,2,1,0:T(8,128)S(1)} %get-tuple-element.92), channel_id=1, source_target_pairs={{16,0},{32,16},{48,32},{64,48},{80,64},{96,80},{112,96},{128,112},... | collective-permute-start | bytes 98312 | tf_op jit(solution)/shard_map/ppermute | solution.py:19
  124.9 6.8 %collective-permute-start.12 = (f32[8,1,8,128]{3,2,1,0:T(8,128)S(1)}, f32[8,1,8,128]{3,2,1,0:T(8,128)S(1)}, u32[]{:S(2)}, u32[]{:S(2)}) collective-permute-start(f32[8,1,8,128]{3,2,1,0:T(8,128)S(1)} %get-tuple-element.93), channel_id=1, source_target_pairs={{0,16},{16,32},{32,48},{48,64},{64,80},{80,96},{96,112},{112,128},... | collective-permute-start | bytes 98312 | tf_op jit(solution)/shard_map/ppermute | solution.py:16
  131.7 5.4 %collective-permute-start.15 = (f32[8,6,1,128]{3,2,1,0:T(1,128)S(1)}, f32[8,6,1,128]{3,2,1,0:T(1,128)S(1)}, u32[]{:S(2)}, u32[]{:S(2)}) collective-permute-start(f32[8,6,1,128]{3,2,1,0:T(1,128)S(1)} %get-tuple-element.80), channel_id=1, source_target_pairs={{4,0},{8,4},{12,8},{0,12},{5,1},{9,5},{13,9},{1,13},{6,2},{10,6},{... | collective-permute-start | bytes 73736 | tf_op jit(solution)/shard_map/ppermute | solution.py:19
  133.6 5.8 %collective-permute-start.14 = (f32[8,6,1,128]{3,2,1,0:T(1,128)S(1)}, f32[8,6,1,128]{3,2,1,0:T(1,128)S(1)}, u32[]{:S(2)}, u32[]{:S(2)}) collective-permute-start(f32[8,6,1,128]{3,2,1,0:T(1,128)S(1)} %get-tuple-element.81), channel_id=1, source_target_pairs={{0,4},{4,8},{8,12},{12,0},{1,5},{5,9},{9,13},{13,1},{2,6},{6,10},{... | collective-permute-start | bytes 73736 | tf_op jit(solution)/shard_map/ppermute | solution.py:16
  139.6 15.3 %collective-permute-start.16 = (f32[8,6,10,1]{3,2,1,0:T(8,128)S(1)}, f32[8,6,10,1]{3,2,1,0:T(8,128)S(1)}, u32[]{:S(2)}, u32[]{:S(2)}) collective-permute-start(f32[8,6,10,1]{3,2,1,0:T(8,128)S(1)} %get-tuple-element.60), channel_id=1, source_target_pairs={{1,0},{2,1},{3,2},{0,3},{5,4},{6,5},{7,6},{4,7},{9,8},{10,9},{11,1... | collective-permute-start | bytes 5768 | tf_op jit(solution)/shard_map/ppermute | solution.py:19
  146.7 9.1 %collective-permute-start.17 = (f32[8,6,10,1]{3,2,1,0:T(8,128)S(1)}, f32[8,6,10,1]{3,2,1,0:T(8,128)S(1)}, u32[]{:S(2)}, u32[]{:S(2)}) collective-permute-start(f32[8,6,10,1]{3,2,1,0:T(8,128)S(1)} %get-tuple-element.61), channel_id=1, source_target_pairs={{0,1},{1,2},{2,3},{3,0},{4,5},{5,6},{6,7},{7,4},{8,9},{9,10},{10,1... | collective-permute-start | bytes 5768 | tf_op jit(solution)/shard_map/ppermute | solution.py:16
  158.5 5.3 %collective-permute-start.19 = (f32[8,1,8,128]{3,2,1,0:T(8,128)S(1)}, f32[8,1,8,128]{3,2,1,0:T(8,128)S(1)}, u32[]{:S(2)}, u32[]{:S(2)}) collective-permute-start(f32[8,1,8,128]{3,2,1,0:T(8,128)S(1)} %get-tuple-element.88), channel_id=1, source_target_pairs={{16,0},{32,16},{48,32},{64,48},{80,64},{96,80},{112,96},{128,112},... | collective-permute-start | bytes 98312 | tf_op jit(solution)/shard_map/ppermute | solution.py:19
  160.4 6.8 %collective-permute-start.18 = (f32[8,1,8,128]{3,2,1,0:T(8,128)S(1)}, f32[8,1,8,128]{3,2,1,0:T(8,128)S(1)}, u32[]{:S(2)}, u32[]{:S(2)}) collective-permute-start(f32[8,1,8,128]{3,2,1,0:T(8,128)S(1)} %get-tuple-element.89), channel_id=1, source_target_pairs={{0,16},{16,32},{32,48},{48,64},{64,80},{80,96},{96,112},{112,128},... | collective-permute-start | bytes 98312 | tf_op jit(solution)/shard_map/ppermute | solution.py:16
  167.2 5.4 %collective-permute-start.21 = (f32[8,6,1,128]{3,2,1,0:T(1,128)S(1)}, f32[8,6,1,128]{3,2,1,0:T(1,128)S(1)}, u32[]{:S(2)}, u32[]{:S(2)}) collective-permute-start(f32[8,6,1,128]{3,2,1,0:T(1,128)S(1)} %get-tuple-element.78), channel_id=1, source_target_pairs={{4,0},{8,4},{12,8},{0,12},{5,1},{9,5},{13,9},{1,13},{6,2},{10,6},{... | collective-permute-start | bytes 73736 | tf_op jit(solution)/shard_map/ppermute | solution.py:19
  169.2 5.8 %collective-permute-start.20 = (f32[8,6,1,128]{3,2,1,0:T(1,128)S(1)}, f32[8,6,1,128]{3,2,1,0:T(1,128)S(1)}, u32[]{:S(2)}, u32[]{:S(2)}) collective-permute-start(f32[8,6,1,128]{3,2,1,0:T(1,128)S(1)} %get-tuple-element.79), channel_id=1, source_target_pairs={{0,4},{4,8},{8,12},{12,0},{1,5},{5,9},{9,13},{13,1},{2,6},{6,10},{... | collective-permute-start | bytes 73736 | tf_op jit(solution)/shard_map/ppermute | solution.py:16
  175.2 15.7 %collective-permute-start.22 = (f32[8,6,10,1]{3,2,1,0:T(8,128)S(1)}, f32[8,6,10,1]{3,2,1,0:T(8,128)S(1)}, u32[]{:S(2)}, u32[]{:S(2)}) collective-permute-start(f32[8,6,10,1]{3,2,1,0:T(8,128)S(1)} %get-tuple-element.58), channel_id=1, source_target_pairs={{1,0},{2,1},{3,2},{0,3},{5,4},{6,5},{7,6},{4,7},{9,8},{10,9},{11,1... | collective-permute-start | bytes 5768 | tf_op jit(solution)/shard_map/ppermute | solution.py:19
  182.3 9.1 %collective-permute-start.23 = (f32[8,6,10,1]{3,2,1,0:T(8,128)S(1)}, f32[8,6,10,1]{3,2,1,0:T(8,128)S(1)}, u32[]{:S(2)}, u32[]{:S(2)}) collective-permute-start(f32[8,6,10,1]{3,2,1,0:T(8,128)S(1)} %get-tuple-element.59), channel_id=1, source_target_pairs={{0,1},{1,2},{2,3},{3,0},{4,5},{5,6},{6,7},{7,4},{8,9},{9,10},{10,1... | collective-permute-start | bytes 5768 | tf_op jit(solution)/shard_map/ppermute | solution.py:16
  193.7 7.4 %collective-permute-start.24 = (f32[2,1,8,128]{3,2,1,0:T(8,128)}, f32[2,1,8,128]{3,2,1,0:T(8,128)S(1)}, u32[]{:S(2)}, u32[]{:S(2)}) collective-permute-start(f32[2,1,8,128]{3,2,1,0:T(8,128)} %get-tuple-element.132), channel_id=1, source_target_pairs={{0,16},{16,32},{32,48},{48,64},{64,80},{80,96},{96,112},{112,128},... | collective-permute-start | bytes 24584 | tf_op jit(solution)/shard_map/ppermute | solution.py:16
  195.6 6.5 %collective-permute-start.25 = (f32[2,1,8,128]{3,2,1,0:T(8,128)}, f32[2,1,8,128]{3,2,1,0:T(8,128)}, u32[]{:S(2)}, u32[]{:S(2)}) collective-permute-start(f32[2,1,8,128]{3,2,1,0:T(8,128)} %get-tuple-element.133), channel_id=1, source_target_pairs={{16,0},{32,16},{48,32},{64,48},{80,64},{96,80},{112,96},{128,112},... | collective-permute-start | bytes 24584 | tf_op jit(solution)/shard_map/ppermute | solution.py:19
  203.5 8.5 %collective-permute-start.26 = (f32[2,6,1,128]{3,2,1,0:T(1,128)}, f32[2,6,1,128]{3,2,1,0:T(1,128)}, u32[]{:S(2)}, u32[]{:S(2)}) collective-permute-start(f32[2,6,1,128]{3,2,1,0:T(1,128)} %get-tuple-element.124), channel_id=1, source_target_pairs={{0,4},{4,8},{8,12},{12,0},{1,5},{5,9},{9,13},{13,1},{2,6},{6,10},{... | collective-permute-start | bytes 18440 | tf_op jit(solution)/shard_map/ppermute | solution.py:16
  205.8 6.3 %collective-permute-start.27 = (f32[2,6,1,128]{3,2,1,0:T(1,128)}, f32[2,6,1,128]{3,2,1,0:T(1,128)}, u32[]{:S(2)}, u32[]{:S(2)}) collective-permute-start(f32[2,6,1,128]{3,2,1,0:T(1,128)} %get-tuple-element.125), channel_id=1, source_target_pairs={{4,0},{8,4},{12,8},{0,12},{5,1},{9,5},{13,9},{1,13},{6,2},{10,6},{... | collective-permute-start | bytes 18440 | tf_op jit(solution)/shard_map/ppermute | solution.py:19
  213.0 10.8 %collective-permute-start.29 = (f32[2,6,10,1]{3,2,1,0:T(8,128)S(1)}, f32[2,6,10,1]{3,2,1,0:T(8,128)S(1)}, u32[]{:S(2)}, u32[]{:S(2)}) collective-permute-start(f32[2,6,10,1]{3,2,1,0:T(8,128)S(1)} %get-tuple-element.108), channel_id=1, source_target_pairs={{0,1},{1,2},{2,3},{3,0},{4,5},{5,6},{6,7},{7,4},{8,9},{9,10},{10,1... | collective-permute-start | bytes 1448 | tf_op jit(solution)/shard_map/ppermute | solution.py:16
  220.6 7.4 %collective-permute-start.28 = (f32[2,6,10,1]{3,2,1,0:T(8,128)S(1)}, f32[2,6,10,1]{3,2,1,0:T(8,128)S(1)}, u32[]{:S(2)}, u32[]{:S(2)}) collective-permute-start(f32[2,6,10,1]{3,2,1,0:T(8,128)S(1)} %get-tuple-element.109), channel_id=1, source_target_pairs={{1,0},{2,1},{3,2},{0,3},{5,4},{6,5},{7,6},{4,7},{9,8},{10,9},{11,1... | collective-permute-start | bytes 1448 | tf_op jit(solution)/shard_map/ppermute | solution.py:19
  238.5 7.9 %collective-permute-start.30 = (f32[2,1,8,128]{3,2,1,0:T(8,128)S(1)}, f32[2,1,8,128]{3,2,1,0:T(8,128)S(1)}, u32[]{:S(2)}, u32[]{:S(2)}) collective-permute-start(f32[2,1,8,128]{3,2,1,0:T(8,128)S(1)} %get-tuple-element.130), channel_id=1, source_target_pairs={{0,16},{16,32},{32,48},{48,64},{64,80},{80,96},{96,112},{112,128},... | collective-permute-start | bytes 24584 | tf_op jit(solution)/shard_map/ppermute | solution.py:16
  240.4 6.4 %collective-permute-start.31 = (f32[2,1,8,128]{3,2,1,0:T(8,128)S(1)}, f32[2,1,8,128]{3,2,1,0:T(8,128)S(1)}, u32[]{:S(2)}, u32[]{:S(2)}) collective-permute-start(f32[2,1,8,128]{3,2,1,0:T(8,128)S(1)} %get-tuple-element.131), channel_id=1, source_target_pairs={{16,0},{32,16},{48,32},{64,48},{80,64},{96,80},{112,96},{128,112},... | collective-permute-start | bytes 24584 | tf_op jit(solution)/shard_map/ppermute | solution.py:19
  246.9 7.5 %collective-permute-start.32 = (f32[2,6,1,128]{3,2,1,0:T(1,128)S(1)}, f32[2,6,1,128]{3,2,1,0:T(1,128)S(1)}, u32[]{:S(2)}, u32[]{:S(2)}) collective-permute-start(f32[2,6,1,128]{3,2,1,0:T(1,128)S(1)} %get-tuple-element.120), channel_id=1, source_target_pairs={{0,4},{4,8},{8,12},{12,0},{1,5},{5,9},{9,13},{13,1},{2,6},{6,10},{... | collective-permute-start | bytes 18440 | tf_op jit(solution)/shard_map/ppermute | solution.py:16
  248.8 5.6 %collective-permute-start.33 = (f32[2,6,1,128]{3,2,1,0:T(1,128)S(1)}, f32[2,6,1,128]{3,2,1,0:T(1,128)S(1)}, u32[]{:S(2)}, u32[]{:S(2)}) collective-permute-start(f32[2,6,1,128]{3,2,1,0:T(1,128)S(1)} %get-tuple-element.121), channel_id=1, source_target_pairs={{4,0},{8,4},{12,8},{0,12},{5,1},{9,5},{13,9},{1,13},{6,2},{10,6},{... | collective-permute-start | bytes 18440 | tf_op jit(solution)/shard_map/ppermute | solution.py:19
  254.6 6.1 %collective-permute-start.35 = (f32[2,6,10,1]{3,2,1,0:T(8,128)S(1)}, f32[2,6,10,1]{3,2,1,0:T(8,128)S(1)}, u32[]{:S(2)}, u32[]{:S(2)}) collective-permute-start(f32[2,6,10,1]{3,2,1,0:T(8,128)S(1)} %get-tuple-element.106), channel_id=1, source_target_pairs={{0,1},{1,2},{2,3},{3,0},{4,5},{5,6},{6,7},{7,4},{8,9},{9,10},{10,1... | collective-permute-start | bytes 1448 | tf_op jit(solution)/shard_map/ppermute | solution.py:16
  258.7 7.4 %collective-permute-start.34 = (f32[2,6,10,1]{3,2,1,0:T(8,128)S(1)}, f32[2,6,10,1]{3,2,1,0:T(8,128)S(1)}, u32[]{:S(2)}, u32[]{:S(2)}) collective-permute-start(f32[2,6,10,1]{3,2,1,0:T(8,128)S(1)} %get-tuple-element.107), channel_id=1, source_target_pairs={{1,0},{2,1},{3,2},{0,3},{5,4},{6,5},{7,6},{4,7},{9,8},{10,9},{11,1... | collective-permute-start | bytes 1448 | tf_op jit(solution)/shard_map/ppermute | solution.py:19
  276.2 7.8 %collective-permute-start.36 = (f32[2,1,8,128]{3,2,1,0:T(8,128)S(1)}, f32[2,1,8,128]{3,2,1,0:T(8,128)S(1)}, u32[]{:S(2)}, u32[]{:S(2)}) collective-permute-start(f32[2,1,8,128]{3,2,1,0:T(8,128)S(1)} %get-tuple-element.128), channel_id=1, source_target_pairs={{0,16},{16,32},{32,48},{48,64},{64,80},{80,96},{96,112},{112,128},... | collective-permute-start | bytes 24584 | tf_op jit(solution)/shard_map/ppermute | solution.py:16
  278.2 6.4 %collective-permute-start.37 = (f32[2,1,8,128]{3,2,1,0:T(8,128)S(1)}, f32[2,1,8,128]{3,2,1,0:T(8,128)S(1)}, u32[]{:S(2)}, u32[]{:S(2)}) collective-permute-start(f32[2,1,8,128]{3,2,1,0:T(8,128)S(1)} %get-tuple-element.129), channel_id=1, source_target_pairs={{16,0},{32,16},{48,32},{64,48},{80,64},{96,80},{112,96},{128,112},... | collective-permute-start | bytes 24584 | tf_op jit(solution)/shard_map/ppermute | solution.py:19
  284.6 8.0 %collective-permute-start.38 = (f32[2,6,1,128]{3,2,1,0:T(1,128)S(1)}, f32[2,6,1,128]{3,2,1,0:T(1,128)S(1)}, u32[]{:S(2)}, u32[]{:S(2)}) collective-permute-start(f32[2,6,1,128]{3,2,1,0:T(1,128)S(1)} %get-tuple-element.116), channel_id=1, source_target_pairs={{0,4},{4,8},{8,12},{12,0},{1,5},{5,9},{9,13},{13,1},{2,6},{6,10},{... | collective-permute-start | bytes 18440 | tf_op jit(solution)/shard_map/ppermute | solution.py:16
  287.7 4.8 %collective-permute-start.39 = (f32[2,6,1,128]{3,2,1,0:T(1,128)S(1)}, f32[2,6,1,128]{3,2,1,0:T(1,128)S(1)}, u32[]{:S(2)}, u32[]{:S(2)}) collective-permute-start(f32[2,6,1,128]{3,2,1,0:T(1,128)S(1)} %get-tuple-element.117), channel_id=1, source_target_pairs={{4,0},{8,4},{12,8},{0,12},{5,1},{9,5},{13,9},{1,13},{6,2},{10,6},{... | collective-permute-start | bytes 18440 | tf_op jit(solution)/shard_map/ppermute | solution.py:19
  292.7 6.2 %collective-permute-start.41 = (f32[2,6,10,1]{3,2,1,0:T(8,128)S(1)}, f32[2,6,10,1]{3,2,1,0:T(8,128)S(1)}, u32[]{:S(2)}, u32[]{:S(2)}) collective-permute-start(f32[2,6,10,1]{3,2,1,0:T(8,128)S(1)} %get-tuple-element.104), channel_id=1, source_target_pairs={{0,1},{1,2},{2,3},{3,0},{4,5},{5,6},{6,7},{7,4},{8,9},{9,10},{10,1... | collective-permute-start | bytes 1448 | tf_op jit(solution)/shard_map/ppermute | solution.py:16
  296.9 7.4 %collective-permute-start.40 = (f32[2,6,10,1]{3,2,1,0:T(8,128)S(1)}, f32[2,6,10,1]{3,2,1,0:T(8,128)S(1)}, u32[]{:S(2)}, u32[]{:S(2)}) collective-permute-start(f32[2,6,10,1]{3,2,1,0:T(8,128)S(1)} %get-tuple-element.105), channel_id=1, source_target_pairs={{1,0},{2,1},{3,2},{0,3},{5,4},{6,5},{7,6},{4,7},{9,8},{10,9},{11,1... | collective-permute-start | bytes 1448 | tf_op jit(solution)/shard_map/ppermute | solution.py:19
  311.7 7.8 %collective-permute-start.42 = (f32[2,1,8,128]{3,2,1,0:T(8,128)S(1)}, f32[2,1,8,128]{3,2,1,0:T(8,128)S(1)}, u32[]{:S(2)}, u32[]{:S(2)}) collective-permute-start(f32[2,1,8,128]{3,2,1,0:T(8,128)S(1)} %get-tuple-element.126), channel_id=1, source_target_pairs={{0,16},{16,32},{32,48},{48,64},{64,80},{80,96},{96,112},{112,128},... | collective-permute-start | bytes 24584 | tf_op jit(solution)/shard_map/ppermute | solution.py:16
  313.7 6.4 %collective-permute-start.43 = (f32[2,1,8,128]{3,2,1,0:T(8,128)S(1)}, f32[2,1,8,128]{3,2,1,0:T(8,128)S(1)}, u32[]{:S(2)}, u32[]{:S(2)}) collective-permute-start(f32[2,1,8,128]{3,2,1,0:T(8,128)S(1)} %get-tuple-element.127), channel_id=1, source_target_pairs={{16,0},{32,16},{48,32},{64,48},{80,64},{96,80},{112,96},{128,112},... | collective-permute-start | bytes 24584 | tf_op jit(solution)/shard_map/ppermute | solution.py:19
  320.1 7.7 %collective-permute-start.44 = (f32[2,6,1,128]{3,2,1,0:T(1,128)S(1)}, f32[2,6,1,128]{3,2,1,0:T(1,128)S(1)}, u32[]{:S(2)}, u32[]{:S(2)}) collective-permute-start(f32[2,6,1,128]{3,2,1,0:T(1,128)S(1)} %get-tuple-element.112), channel_id=1, source_target_pairs={{0,4},{4,8},{8,12},{12,0},{1,5},{5,9},{9,13},{13,1},{2,6},{6,10},{... | collective-permute-start | bytes 18440 | tf_op jit(solution)/shard_map/ppermute | solution.py:16
  323.7 4.4 collective-permute-start.45
  328.2 6.7 %collective-permute-start.47 = (f32[2,6,10,1]{3,2,1,0:T(8,128)S(1)}, f32[2,6,10,1]{3,2,1,0:T(8,128)S(1)}, u32[]{:S(2)}, u32[]{:S(2)}) collective-permute-start(f32[2,6,10,1]{3,2,1,0:T(8,128)S(1)} %get-tuple-element.102), channel_id=1, source_target_pairs={{0,1},{1,2},{2,3},{3,0},{4,5},{5,6},{6,7},{7,4},{8,9},{9,10},{10,1... | collective-permute-start | bytes 1448 | tf_op jit(solution)/shard_map/ppermute | solution.py:16
  332.9 7.4 %collective-permute-start.46 = (f32[2,6,10,1]{3,2,1,0:T(8,128)S(1)}, f32[2,6,10,1]{3,2,1,0:T(8,128)S(1)}, u32[]{:S(2)}, u32[]{:S(2)}) collective-permute-start(f32[2,6,10,1]{3,2,1,0:T(8,128)S(1)} %get-tuple-element.103), channel_id=1, source_target_pairs={{1,0},{2,1},{3,2},{0,3},{5,4},{6,5},{7,6},{4,7},{9,8},{10,9},{11,1... | collective-permute-start | bytes 1448 | tf_op jit(solution)/shard_map/ppermute | solution.py:19
  (111 other events, 1441.8 us)
where the time goes:
time: 456 us; the launch traced here: 452 us
  starting transfers between devices  174 us (38%)
  blocking collectives  138 us (30%)
  waiting for transfers between devices  71.5 us (16%)
  other arithmetic  25.7 us (6%)
  matrix products  21.9 us (5%)
  local copies, waits for them, and re-layouts  17.4 us (4%)
    psum x1, blocking collectives, per_device(): lax.psum((sum_w_in, sum_b_in, sum_w_mid, sum_b_mid, sum_w_out, sum_b_out,...  104 us
    ppermute x24, starting transfers between devices, extended(): lax.ppermute(lax.slice_in_dim(block, 0, width, axis=dim), axis, backward)  96.7 us
    ppermute x24, starting transfers between devices, extended(): lax.ppermute(lax.slice_in_dim(block, block.shape[dim] - width, None, axis...  77 us
    ppermute x24, waiting for transfers between devices, extended(): lax.ppermute(lax.slice_in_dim(block, 0, width, axis=dim), axis, backward)  43.1 us
    ppermute x24, waiting for transfers between devices, extended(): lax.ppermute(lax.slice_in_dim(block, block.shape[dim] - width, None, axis...  28.4 us
    unnamed x1, blocking collectives  13.4 us
  transfers between devices with their start and end apart: 48, of which 25 were waited for; matrix products, arithmetic and copies ran while one was open for 1% of the time, Pallas kernels for 0%

commit v1 on v0

--- a/solution.py
+++ b/solution.py
@@ -172,8 +172,11 @@
     start_sensitivity = adjoint * (2.0 * total_cells)
     sum_w_in, sum_b_in, sum_w_mid, sum_b_mid, sum_w_out, sum_b_out = grad_sums
     summed = lax.psum(
-        (sum_w_in, sum_b_in, sum_w_mid, sum_b_mid, sum_w_out, sum_b_out, loss_part),
-        ("blk", "gy", "rep"),
+        lax.psum(
+            (sum_w_in, sum_b_in, sum_w_mid, sum_b_mid, sum_w_out, sum_b_out, loss_part),
+            ("gy", "rep"),
+        ),
+        "blk",
     )
     position = lax.axis_index("rep")
     share_width = w_in.shape[0]

time: 456 us -> 542 us (1.19)
  the two profiles are of different devices: /device:TPU:1 before, /device:TPU:8 now
where the time goes in v1:
time: 542 us; the launch traced here: 539 us
  blocking collectives  223 us (41%)
  starting transfers between devices  163 us (30%)
  waiting for transfers between devices  83.6 us (15%)
  other arithmetic  25.6 us (5%)
  matrix products  22 us (4%)
  local copies, waits for them, and re-layouts  17.4 us (3%)
    psum x1, blocking collectives, per_device(): lax.psum(lax.psum((sum_w_in, sum_b_in, sum_w_mid, sum_b_mid, sum_w_out, s...  123 us
    ppermute x24, starting transfers between devices, extended(): lax.ppermute(lax.slice_in_dim(block, 0, width, axis=dim), axis, backward)  99.5 us
    psum x1, blocking collectives, per_device(): lax.psum((sum_w_in, sum_b_in, sum_w_mid, sum_b_mid, sum_w_out, sum_b_out,...  71.4 us
    ppermute x24, starting transfers between devices, extended(): lax.ppermute(lax.slice_in_dim(block, block.shape[dim] - width, None, axis...  63.6 us
    ppermute x24, waiting for transfers between devices, extended(): lax.ppermute(lax.slice_in_dim(block, block.shape[dim] - width, None, axis...  54 us
    ppermute x24, waiting for transfers between devices, extended(): lax.ppermute(lax.slice_in_dim(block, 0, width, axis=dim), axis, backward)  29.7 us
  transfers between devices with their start and end apart: 48, of which 30 were waited for; matrix products, arithmetic and copies ran while one was open for 1% of the time, Pallas kernels for 0%

profile of v1, /device:TPU:8, one launch (start us, length us, event | category | flops | bytes accessed | tf_op | source)
XLA Modules:
  0.0 539.4 jit_solution(2868343613934609087)
XLA Ops:
  5.0 9.2 %all-reduce.4 = (bf16[64]{0:T(256)(128)(2,1)S(1)}, bf16[64]{0:T(256)(128)(2,1)S(1)}) all-reduce(bf16[64]{0:T(256)(128)(2,1)S(1)} %dynamic-update-slice.1, bf16[64]{0:T(256)(128)(2,1)S(1)} %dynamic-update-slice), channel_id=1, replica_groups=mesh['blk'=32,'gy'=4,'rep'=4] {'rep'}, use_global_device_ids=true, to_apply=%add.1 | all-reduce | flops 128 | bytes 512
  16.3 6.7 %all-gather = bf16[4,16,6]{1,2,0:T(8,128)(2,1)S(1)} all-gather(bf16[1,16,6]{1,2,0:T(8,128)(2,1)S(1)} %convert_bitcast_fusion.4), channel_id=1, replica_groups=mesh['blk'=32,'gy'=4,'rep'=4] {'rep'}, dimensions={0}, use_global_device_ids=true | all-gather | bytes 960 | tf_op jit(solution)/shard_map/all_gather | solution.py:123
  23.1 6.7 %all_gather.17 = bf16[64,64]{1,0:T(8,128)(2,1)S(1)} all-gather(bf16[16,64]{1,0:T(8,128)(2,1)S(1)} %convert_element_type.210), channel_id=1, replica_groups=mesh['blk'=32,'gy'=4,'rep'=4] {'rep'}, dimensions={0}, use_global_device_ids=true | all-gather | bytes 10240 | tf_op jit(solution)/shard_map/all_gather | solution.py:121
  29.7 6.7 %all_gather.15 = bf16[64,10]{1,0:T(8,128)(2,1)S(1)} all-gather(bf16[16,10]{1,0:T(8,128)(2,1)S(1)} %convert_element_type.206), channel_id=1, replica_groups=mesh['blk'=32,'gy'=4,'rep'=4] {'rep'}, dimensions={0}, use_global_device_ids=true | all-gather | bytes 1600 | tf_op jit(solution)/shard_map/all_gather | solution.py:119
  39.5 12.2 %collective-permute-start.1 = (f32[8,1,8,128]{3,2,1,0:T(8,128)S(1)}, f32[8,1,8,128]{3,2,1,0:T(8,128)S(1)}, u32[]{:S(2)}, u32[]{:S(2)}) collective-permute-start(f32[8,1,8,128]{3,2,1,0:T(8,128)S(1)} %get-tuple-element.107), channel_id=1, source_target_pairs={{16,0},{32,16},{48,32},{64,48},{80,64},{96,80},{112,96},{128,112},... | collective-permute-start | bytes 98312 | tf_op jit(solution)/shard_map/ppermute | solution.py:19
  53.7 6.0 %collective-permute-done = f32[8,1,8,128]{3,2,1,0:T(8,128)S(1)} collective-permute-done((f32[8,1,8,128]{3,2,1,0:T(8,128)S(1)}, f32[8,1,8,128]{3,2,1,0:T(8,128)S(1)}, u32[]{:S(2)}, u32[]{:S(2)}) %collective-permute-start) | collective-permute-done | bytes 32800 | tf_op jit(solution)/shard_map/ppermute | solution.py:16
  59.7 4.7 collective-permute-start.3
  66.4 4.9 collective-permute-done.2
  73.5 2.4 collective-permute-start.5
  75.9 5.1 collective-permute-done.4
  81.0 3.1 collective-permute-done.5
  88.9 3.9 collective-permute-start.6
  92.9 4.0 collective-permute-done.6
  98.8 3.9 collective-permute-start.8
  102.8 2.9 collective-permute-done.8
  107.9 2.4 collective-permute-start.11
  110.4 2.8 collective-permute-done.10
  113.2 7.5 %collective-permute-done.11 = f32[8,6,10,1]{3,2,1,0:T(8,128)S(1)} collective-permute-done((f32[8,6,10,1]{3,2,1,0:T(8,128)S(1)}, f32[8,6,10,1]{3,2,1,0:T(8,128)S(1)}, u32[]{:S(2)}, u32[]{:S(2)}) %collective-permute-start.11) | collective-permute-done | bytes 1952 | tf_op jit(solution)/shard_map/ppermute | solution.py:16
  125.9 3.6 collective-permute-start.12
  129.6 4.3 collective-permute-done.12
  135.8 3.9 collective-permute-start.14
  139.8 2.9 collective-permute-done.14
  144.9 2.4 collective-permute-start.17
  147.4 5.2 collective-permute-done.16
  152.6 2.9 collective-permute-done.17
  160.1 3.9 collective-permute-start.18
  164.1 4.0 collective-permute-done.18
  170.2 3.7 collective-permute-start.20
  174.0 3.1 collective-permute-done.20
  181.8 2.8 collective-permute-done.22
  184.6 7.5 %collective-permute-done.23 = f32[8,6,10,1]{3,2,1,0:T(8,128)S(1)} collective-permute-done((f32[8,6,10,1]{3,2,1,0:T(8,128)S(1)}, f32[8,6,10,1]{3,2,1,0:T(8,128)S(1)}, u32[]{:S(2)}, u32[]{:S(2)}) %collective-permute-start.23) | collective-permute-done | bytes 1952 | tf_op jit(solution)/shard_map/ppermute | solution.py:16
  196.3 6.0 %collective-permute-start.25 = (f32[2,1,8,128]{3,2,1,0:T(8,128)}, f32[2,1,8,128]{3,2,1,0:T(8,128)}, u32[]{:S(2)}, u32[]{:S(2)}) collective-permute-start(f32[2,1,8,128]{3,2,1,0:T(8,128)} %get-tuple-element.140), channel_id=1, source_target_pairs={{16,0},{32,16},{48,32},{64,48},{80,64},{96,80},{112,96},{128,112},... | collective-permute-start | bytes 24584 | tf_op jit(solution)/shard_map/ppermute | solution.py:19
  205.4 2.5 collective-permute-start.26
  207.9 4.5 collective-permute-start.27
  217.3 5.3 collective-permute-start.28
  237.2 6.6 %collective-permute-start.31 = (f32[2,1,8,128]{3,2,1,0:T(8,128)S(1)}, f32[2,1,8,128]{3,2,1,0:T(8,128)S(1)}, u32[]{:S(2)}, u32[]{:S(2)}) collective-permute-start(f32[2,1,8,128]{3,2,1,0:T(8,128)S(1)} %get-tuple-element.138), channel_id=1, source_target_pairs={{16,0},{32,16},{48,32},{64,48},{80,64},{96,80},{112,96},{128,112},... | collective-permute-start | bytes 24584 | tf_op jit(solution)/shard_map/ppermute | solution.py:19
  247.0 5.1 collective-permute-start.33
  255.5 5.1 collective-permute-start.34
  274.9 6.4 %collective-permute-start.37 = (f32[2,1,8,128]{3,2,1,0:T(8,128)S(1)}, f32[2,1,8,128]{3,2,1,0:T(8,128)S(1)}, u32[]{:S(2)}, u32[]{:S(2)}) collective-permute-start(f32[2,1,8,128]{3,2,1,0:T(8,128)S(1)} %get-tuple-element.136), channel_id=1, source_target_pairs={{16,0},{32,16},{48,32},{64,48},{80,64},{96,80},{112,96},{128,112},... | collective-permute-start | bytes 24584 | tf_op jit(solution)/shard_map/ppermute | solution.py:19
  282.7 3.4 collective-permute-start.38
  286.1 3.9 collective-permute-start.39
  293.7 5.1 collective-permute-start.40
  310.4 6.4 %collective-permute-start.43 = (f32[2,1,8,128]{3,2,1,0:T(8,128)S(1)}, f32[2,1,8,128]{3,2,1,0:T(8,128)S(1)}, u32[]{:S(2)}, u32[]{:S(2)}) collective-permute-start(f32[2,1,8,128]{3,2,1,0:T(8,128)S(1)} %get-tuple-element.134), channel_id=1, source_target_pairs={{16,0},{32,16},{48,32},{64,48},{80,64},{96,80},{112,96},{128,112},... | collective-permute-start | bytes 24584 | tf_op jit(solution)/shard_map/ppermute | solution.py:19
  318.2 3.9 collective-permute-start.44
  322.1 3.1 collective-permute-start.45
  329.7 5.1 collective-permute-start.46
  340.5 71.4 %all-reduce.3 = (f32[]{:T(128)}, f32[64,10]{1,0:T(8,128)S(1)}, f32[64]{0:T(128)S(1)}, f32[64,64]{1,0:T(8,128)S(1)}, f32[64]{0:T(128)S(1)}, /*index=5*/f32[6,64]{1,0:T(8,128)S(1)}, f32[6]{0:T(128)S(1)}) all-reduce(f32[]{:T(128)S(6)} %div.30, ...), channel_id=1, replica_groups=mesh['blk'=32,'gy'=4,'rep'=4] {'gy','rep'}, use_global_device_ids=true, to_apply=%region_1.0 | all-reduce | flops 5255 | bytes 42040 | tf_op jit(solution)/shard_map/psum | solution.py:175
  411.9 122.8 %all-reduce.2 = (f32[]{:T(128)}, f32[64,10]{1,0:T(8,128)S(1)}, f32[64]{0:T(128)S(1)}, f32[64,64]{1,0:T(8,128)S(1)}, f32[64]{0:T(128)S(1)}, /*index=5*/f32[6,64]{1,0:T(8,128)S(1)}, f32[6]{0:T(128)}) all-reduce(f32[]{:T(128)} %get-tuple-element.16, ...), channel_id=1, replica_groups=mesh['blk'=32,'gy'=4,'rep'=4] {'blk'}, use_global_device_ids=true, to_apply=%region_2.0 | all-reduce | flops 5255 | bytes 42040 | tf_op jit(solution)/shard_map/psum | solution.py:174
  (433 shorter events, 122.9 us)
Async XLA Ops:
  39.5 14.1 %collective-permute-start.1 = (f32[8,1,8,128]{3,2,1,0:T(8,128)S(1)}, f32[8,1,8,128]{3,2,1,0:T(8,128)S(1)}, u32[]{:S(2)}, u32[]{:S(2)}) collective-permute-start(f32[8,1,8,128]{3,2,1,0:T(8,128)S(1)} %get-tuple-element.107), channel_id=1, source_target_pairs={{16,0},{32,16},{48,32},{64,48},{80,64},{96,80},{112,96},{128,112},... | collective-permute-start | bytes 98312 | tf_op jit(solution)/shard_map/ppermute | solution.py:19
  51.7 7.9 %collective-permute-start = (f32[8,1,8,128]{3,2,1,0:T(8,128)S(1)}, f32[8,1,8,128]{3,2,1,0:T(8,128)S(1)}, u32[]{:S(2)}, u32[]{:S(2)}) collective-permute-start(f32[8,1,8,128]{3,2,1,0:T(8,128)S(1)} %get-tuple-element.108), channel_id=1, source_target_pairs={{0,16},{16,32},{32,48},{48,64},{64,80},{80,96},{96,112},{112,128},... | collective-permute-start | bytes 98312 | tf_op jit(solution)/shard_map/ppermute | solution.py:16
  59.7 6.7 %collective-permute-start.3 = (f32[8,6,1,128]{3,2,1,0:T(1,128)S(1)}, f32[8,6,1,128]{3,2,1,0:T(1,128)S(1)}, u32[]{:S(2)}, u32[]{:S(2)}) collective-permute-start(f32[8,6,1,128]{3,2,1,0:T(1,128)S(1)} %get-tuple-element.91), channel_id=1, source_target_pairs={{4,0},{8,4},{12,8},{0,12},{5,1},{9,5},{13,9},{1,13},{6,2},{10,6},{... | collective-permute-start | bytes 73736 | tf_op jit(solution)/shard_map/ppermute | solution.py:19
  64.4 6.9 %collective-permute-start.2 = (f32[8,6,1,128]{3,2,1,0:T(1,128)S(1)}, f32[8,6,1,128]{3,2,1,0:T(1,128)S(1)}, u32[]{:S(2)}, u32[]{:S(2)}) collective-permute-start(f32[8,6,1,128]{3,2,1,0:T(1,128)S(1)} %get-tuple-element.92), channel_id=1, source_target_pairs={{0,4},{4,8},{8,12},{12,0},{1,5},{5,9},{9,13},{13,1},{2,6},{6,10},{... | collective-permute-start | bytes 73736 | tf_op jit(solution)/shard_map/ppermute | solution.py:16
  71.6 9.4 %collective-permute-start.4 = (f32[8,6,10,1]{3,2,1,0:T(8,128)S(1)}, f32[8,6,10,1]{3,2,1,0:T(8,128)S(1)}, u32[]{:S(2)}, u32[]{:S(2)}) collective-permute-start(f32[8,6,10,1]{3,2,1,0:T(8,128)S(1)} %get-tuple-element.71), channel_id=1, source_target_pairs={{1,0},{2,1},{3,2},{0,3},{5,4},{6,5},{7,6},{4,7},{9,8},{10,9},{11,1... | collective-permute-start | bytes 5768 | tf_op jit(solution)/shard_map/ppermute | solution.py:19
  73.5 10.6 %collective-permute-start.5 = (f32[8,6,10,1]{3,2,1,0:T(8,128)S(1)}, f32[8,6,10,1]{3,2,1,0:T(8,128)S(1)}, u32[]{:S(2)}, u32[]{:S(2)}) collective-permute-start(f32[8,6,10,1]{3,2,1,0:T(8,128)S(1)} %get-tuple-element.72), channel_id=1, source_target_pairs={{0,1},{1,2},{2,3},{3,0},{4,5},{5,6},{6,7},{7,4},{8,9},{9,10},{10,1... | collective-permute-start | bytes 5768 | tf_op jit(solution)/shard_map/ppermute | solution.py:16
  87.0 5.9 %collective-permute-start.7 = (f32[8,1,8,128]{3,2,1,0:T(8,128)S(1)}, f32[8,1,8,128]{3,2,1,0:T(8,128)S(1)}, u32[]{:S(2)}, u32[]{:S(2)}) collective-permute-start(f32[8,1,8,128]{3,2,1,0:T(8,128)S(1)} %get-tuple-element.103), channel_id=1, source_target_pairs={{16,0},{32,16},{48,32},{64,48},{80,64},{96,80},{112,96},{128,112},... | collective-permute-start | bytes 98312 | tf_op jit(solution)/shard_map/ppermute | solution.py:19
  88.9 7.9 %collective-permute-start.6 = (f32[8,1,8,128]{3,2,1,0:T(8,128)S(1)}, f32[8,1,8,128]{3,2,1,0:T(8,128)S(1)}, u32[]{:S(2)}, u32[]{:S(2)}) collective-permute-start(f32[8,1,8,128]{3,2,1,0:T(8,128)S(1)} %get-tuple-element.104), channel_id=1, source_target_pairs={{0,16},{16,32},{32,48},{48,64},{64,80},{80,96},{96,112},{112,128},... | collective-permute-start | bytes 98312 | tf_op jit(solution)/shard_map/ppermute | solution.py:16
  96.9 5.9 %collective-permute-start.9 = (f32[8,6,1,128]{3,2,1,0:T(1,128)S(1)}, f32[8,6,1,128]{3,2,1,0:T(1,128)S(1)}, u32[]{:S(2)}, u32[]{:S(2)}) collective-permute-start(f32[8,6,1,128]{3,2,1,0:T(1,128)S(1)} %get-tuple-element.89), channel_id=1, source_target_pairs={{4,0},{8,4},{12,8},{0,12},{5,1},{9,5},{13,9},{1,13},{6,2},{10,6},{... | collective-permute-start | bytes 73736 | tf_op jit(solution)/shard_map/ppermute | solution.py:19
  98.8 6.9 %collective-permute-start.8 = (f32[8,6,1,128]{3,2,1,0:T(1,128)S(1)}, f32[8,6,1,128]{3,2,1,0:T(1,128)S(1)}, u32[]{:S(2)}, u32[]{:S(2)}) collective-permute-start(f32[8,6,1,128]{3,2,1,0:T(1,128)S(1)} %get-tuple-element.90), channel_id=1, source_target_pairs={{0,4},{4,8},{8,12},{12,0},{1,5},{5,9},{9,13},{13,1},{2,6},{6,10},{... | collective-permute-start | bytes 73736 | tf_op jit(solution)/shard_map/ppermute | solution.py:16
  106.0 7.2 %collective-permute-start.10 = (f32[8,6,10,1]{3,2,1,0:T(8,128)S(1)}, f32[8,6,10,1]{3,2,1,0:T(8,128)S(1)}, u32[]{:S(2)}, u32[]{:S(2)}) collective-permute-start(f32[8,6,10,1]{3,2,1,0:T(8,128)S(1)} %get-tuple-element.69), channel_id=1, source_target_pairs={{1,0},{2,1},{3,2},{0,3},{5,4},{6,5},{7,6},{4,7},{9,8},{10,9},{11,1... | collective-permute-start | bytes 5768 | tf_op jit(solution)/shard_map/ppermute | solution.py:19
  107.9 12.8 %collective-permute-start.11 = (f32[8,6,10,1]{3,2,1,0:T(8,128)S(1)}, f32[8,6,10,1]{3,2,1,0:T(8,128)S(1)}, u32[]{:S(2)}, u32[]{:S(2)}) collective-permute-start(f32[8,6,10,1]{3,2,1,0:T(8,128)S(1)} %get-tuple-element.70), channel_id=1, source_target_pairs={{0,1},{1,2},{2,3},{3,0},{4,5},{5,6},{6,7},{7,4},{8,9},{9,10},{10,1... | collective-permute-start | bytes 5768 | tf_op jit(solution)/shard_map/ppermute | solution.py:16
  123.7 5.9 %collective-permute-start.13 = (f32[8,1,8,128]{3,2,1,0:T(8,128)S(1)}, f32[8,1,8,128]{3,2,1,0:T(8,128)S(1)}, u32[]{:S(2)}, u32[]{:S(2)}) collective-permute-start(f32[8,1,8,128]{3,2,1,0:T(8,128)S(1)} %get-tuple-element.99), channel_id=1, source_target_pairs={{16,0},{32,16},{48,32},{64,48},{80,64},{96,80},{112,96},{128,112},... | collective-permute-start | bytes 98312 | tf_op jit(solution)/shard_map/ppermute | solution.py:19
  125.9 7.9 %collective-permute-start.12 = (f32[8,1,8,128]{3,2,1,0:T(8,128)S(1)}, f32[8,1,8,128]{3,2,1,0:T(8,128)S(1)}, u32[]{:S(2)}, u32[]{:S(2)}) collective-permute-start(f32[8,1,8,128]{3,2,1,0:T(8,128)S(1)} %get-tuple-element.100), channel_id=1, source_target_pairs={{0,16},{16,32},{32,48},{48,64},{64,80},{80,96},{96,112},{112,128},... | collective-permute-start | bytes 98312 | tf_op jit(solution)/shard_map/ppermute | solution.py:16
  133.9 5.9 %collective-permute-start.15 = (f32[8,6,1,128]{3,2,1,0:T(1,128)S(1)}, f32[8,6,1,128]{3,2,1,0:T(1,128)S(1)}, u32[]{:S(2)}, u32[]{:S(2)}) collective-permute-start(f32[8,6,1,128]{3,2,1,0:T(1,128)S(1)} %get-tuple-element.87), channel_id=1, source_target_pairs={{4,0},{8,4},{12,8},{0,12},{5,1},{9,5},{13,9},{1,13},{6,2},{10,6},{... | collective-permute-start | bytes 73736 | tf_op jit(solution)/shard_map/ppermute | solution.py:19
  135.8 6.9 %collective-permute-start.14 = (f32[8,6,1,128]{3,2,1,0:T(1,128)S(1)}, f32[8,6,1,128]{3,2,1,0:T(1,128)S(1)}, u32[]{:S(2)}, u32[]{:S(2)}) collective-permute-start(f32[8,6,1,128]{3,2,1,0:T(1,128)S(1)} %get-tuple-element.88), channel_id=1, source_target_pairs={{0,4},{4,8},{8,12},{12,0},{1,5},{5,9},{9,13},{13,1},{2,6},{6,10},{... | collective-permute-start | bytes 73736 | tf_op jit(solution)/shard_map/ppermute | solution.py:16
  143.0 9.6 %collective-permute-start.16 = (f32[8,6,10,1]{3,2,1,0:T(8,128)S(1)}, f32[8,6,10,1]{3,2,1,0:T(8,128)S(1)}, u32[]{:S(2)}, u32[]{:S(2)}) collective-permute-start(f32[8,6,10,1]{3,2,1,0:T(8,128)S(1)} %get-tuple-element.67), channel_id=1, source_target_pairs={{1,0},{2,1},{3,2},{0,3},{5,4},{6,5},{7,6},{4,7},{9,8},{10,9},{11,1... | collective-permute-start | bytes 5768 | tf_op jit(solution)/shard_map/ppermute | solution.py:19
  144.9 10.6 %collective-permute-start.17 = (f32[8,6,10,1]{3,2,1,0:T(8,128)S(1)}, f32[8,6,10,1]{3,2,1,0:T(8,128)S(1)}, u32[]{:S(2)}, u32[]{:S(2)}) collective-permute-start(f32[8,6,10,1]{3,2,1,0:T(8,128)S(1)} %get-tuple-element.68), channel_id=1, source_target_pairs={{0,1},{1,2},{2,3},{3,0},{4,5},{5,6},{6,7},{7,4},{8,9},{9,10},{10,1... | collective-permute-start | bytes 5768 | tf_op jit(solution)/shard_map/ppermute | solution.py:16
  158.2 5.9 %collective-permute-start.19 = (f32[8,1,8,128]{3,2,1,0:T(8,128)S(1)}, f32[8,1,8,128]{3,2,1,0:T(8,128)S(1)}, u32[]{:S(2)}, u32[]{:S(2)}) collective-permute-start(f32[8,1,8,128]{3,2,1,0:T(8,128)S(1)} %get-tuple-element.95), channel_id=1, source_target_pairs={{16,0},{32,16},{48,32},{64,48},{80,64},{96,80},{112,96},{128,112},... | collective-permute-start | bytes 98312 | tf_op jit(solution)/shard_map/ppermute | solution.py:19
  160.1 7.9 %collective-permute-start.18 = (f32[8,1,8,128]{3,2,1,0:T(8,128)S(1)}, f32[8,1,8,128]{3,2,1,0:T(8,128)S(1)}, u32[]{:S(2)}, u32[]{:S(2)}) collective-permute-start(f32[8,1,8,128]{3,2,1,0:T(8,128)S(1)} %get-tuple-element.96), channel_id=1, source_target_pairs={{0,16},{16,32},{32,48},{48,64},{64,80},{80,96},{96,112},{112,128},... | collective-permute-start | bytes 98312 | tf_op jit(solution)/shard_map/ppermute | solution.py:16
  168.1 5.9 %collective-permute-start.21 = (f32[8,6,1,128]{3,2,1,0:T(1,128)S(1)}, f32[8,6,1,128]{3,2,1,0:T(1,128)S(1)}, u32[]{:S(2)}, u32[]{:S(2)}) collective-permute-start(f32[8,6,1,128]{3,2,1,0:T(1,128)S(1)} %get-tuple-element.85), channel_id=1, source_target_pairs={{4,0},{8,4},{12,8},{0,12},{5,1},{9,5},{13,9},{1,13},{6,2},{10,6},{... | collective-permute-start | bytes 73736 | tf_op jit(solution)/shard_map/ppermute | solution.py:19
  170.2 6.9 %collective-permute-start.20 = (f32[8,6,1,128]{3,2,1,0:T(1,128)S(1)}, f32[8,6,1,128]{3,2,1,0:T(1,128)S(1)}, u32[]{:S(2)}, u32[]{:S(2)}) collective-permute-start(f32[8,6,1,128]{3,2,1,0:T(1,128)S(1)} %get-tuple-element.86), channel_id=1, source_target_pairs={{0,4},{4,8},{8,12},{12,0},{1,5},{5,9},{9,13},{13,1},{2,6},{6,10},{... | collective-permute-start | bytes 73736 | tf_op jit(solution)/shard_map/ppermute | solution.py:16
  177.4 7.2 %collective-permute-start.22 = (f32[8,6,10,1]{3,2,1,0:T(8,128)S(1)}, f32[8,6,10,1]{3,2,1,0:T(8,128)S(1)}, u32[]{:S(2)}, u32[]{:S(2)}) collective-permute-start(f32[8,6,10,1]{3,2,1,0:T(8,128)S(1)} %get-tuple-element.65), channel_id=1, source_target_pairs={{1,0},{2,1},{3,2},{0,3},{5,4},{6,5},{7,6},{4,7},{9,8},{10,9},{11,1... | collective-permute-start | bytes 5768 | tf_op jit(solution)/shard_map/ppermute | solution.py:19
  179.3 12.8 %collective-permute-start.23 = (f32[8,6,10,1]{3,2,1,0:T(8,128)S(1)}, f32[8,6,10,1]{3,2,1,0:T(8,128)S(1)}, u32[]{:S(2)}, u32[]{:S(2)}) collective-permute-start(f32[8,6,10,1]{3,2,1,0:T(8,128)S(1)} %get-tuple-element.66), channel_id=1, source_target_pairs={{0,1},{1,2},{2,3},{3,0},{4,5},{5,6},{6,7},{7,4},{8,9},{9,10},{10,1... | collective-permute-start | bytes 5768 | tf_op jit(solution)/shard_map/ppermute | solution.py:16
  194.4 8.0 %collective-permute-start.24 = (f32[2,1,8,128]{3,2,1,0:T(8,128)}, f32[2,1,8,128]{3,2,1,0:T(8,128)S(1)}, u32[]{:S(2)}, u32[]{:S(2)}) collective-permute-start(f32[2,1,8,128]{3,2,1,0:T(8,128)} %get-tuple-element.139), channel_id=1, source_target_pairs={{0,16},{16,32},{32,48},{48,64},{64,80},{80,96},{96,112},{112,128},... | collective-permute-start | bytes 24584 | tf_op jit(solution)/shard_map/ppermute | solution.py:16
  196.3 7.6 %collective-permute-start.25 = (f32[2,1,8,128]{3,2,1,0:T(8,128)}, f32[2,1,8,128]{3,2,1,0:T(8,128)}, u32[]{:S(2)}, u32[]{:S(2)}) collective-permute-start(f32[2,1,8,128]{3,2,1,0:T(8,128)} %get-tuple-element.140), channel_id=1, source_target_pairs={{16,0},{32,16},{48,32},{64,48},{80,64},{96,80},{112,96},{128,112},... | collective-permute-start | bytes 24584 | tf_op jit(solution)/shard_map/ppermute | solution.py:19
  205.4 9.1 %collective-permute-start.26 = (f32[2,6,1,128]{3,2,1,0:T(1,128)}, f32[2,6,1,128]{3,2,1,0:T(1,128)}, u32[]{:S(2)}, u32[]{:S(2)}) collective-permute-start(f32[2,6,1,128]{3,2,1,0:T(1,128)} %get-tuple-element.131), channel_id=1, source_target_pairs={{0,4},{4,8},{8,12},{12,0},{1,5},{5,9},{9,13},{13,1},{2,6},{6,10},{... | collective-permute-start | bytes 18440 | tf_op jit(solution)/shard_map/ppermute | solution.py:16
  207.9 6.6 %collective-permute-start.27 = (f32[2,6,1,128]{3,2,1,0:T(1,128)}, f32[2,6,1,128]{3,2,1,0:T(1,128)}, u32[]{:S(2)}, u32[]{:S(2)}) collective-permute-start(f32[2,6,1,128]{3,2,1,0:T(1,128)} %get-tuple-element.132), channel_id=1, source_target_pairs={{4,0},{8,4},{12,8},{0,12},{5,1},{9,5},{13,9},{1,13},{6,2},{10,6},{... | collective-permute-start | bytes 18440 | tf_op jit(solution)/shard_map/ppermute | solution.py:19
  215.4 8.3 %collective-permute-start.29 = (f32[2,6,10,1]{3,2,1,0:T(8,128)S(1)}, f32[2,6,10,1]{3,2,1,0:T(8,128)S(1)}, u32[]{:S(2)}, u32[]{:S(2)}) collective-permute-start(f32[2,6,10,1]{3,2,1,0:T(8,128)S(1)} %get-tuple-element.115), channel_id=1, source_target_pairs={{0,1},{1,2},{2,3},{3,0},{4,5},{5,6},{6,7},{7,4},{8,9},{9,10},{10,1... | collective-permute-start | bytes 1448 | tf_op jit(solution)/shard_map/ppermute | solution.py:16
  217.3 7.3 %collective-permute-start.28 = (f32[2,6,10,1]{3,2,1,0:T(8,128)S(1)}, f32[2,6,10,1]{3,2,1,0:T(8,128)S(1)}, u32[]{:S(2)}, u32[]{:S(2)}) collective-permute-start(f32[2,6,10,1]{3,2,1,0:T(8,128)S(1)} %get-tuple-element.116), channel_id=1, source_target_pairs={{1,0},{2,1},{3,2},{0,3},{5,4},{6,5},{7,6},{4,7},{9,8},{10,9},{11,1... | collective-permute-start | bytes 1448 | tf_op jit(solution)/shard_map/ppermute | solution.py:19
  235.2 8.8 %collective-permute-start.30 = (f32[2,1,8,128]{3,2,1,0:T(8,128)S(1)}, f32[2,1,8,128]{3,2,1,0:T(8,128)S(1)}, u32[]{:S(2)}, u32[]{:S(2)}) collective-permute-start(f32[2,1,8,128]{3,2,1,0:T(8,128)S(1)} %get-tuple-element.137), channel_id=1, source_target_pairs={{0,16},{16,32},{32,48},{48,64},{64,80},{80,96},{96,112},{112,128},... | collective-permute-start | bytes 24584 | tf_op jit(solution)/shard_map/ppermute | solution.py:16
  237.2 7.9 %collective-permute-start.31 = (f32[2,1,8,128]{3,2,1,0:T(8,128)S(1)}, f32[2,1,8,128]{3,2,1,0:T(8,128)S(1)}, u32[]{:S(2)}, u32[]{:S(2)}) collective-permute-start(f32[2,1,8,128]{3,2,1,0:T(8,128)S(1)} %get-tuple-element.138), channel_id=1, source_target_pairs={{16,0},{32,16},{48,32},{64,48},{80,64},{96,80},{112,96},{128,112},... | collective-permute-start | bytes 24584 | tf_op jit(solution)/shard_map/ppermute | solution.py:19
  245.1 8.0 %collective-permute-start.32 = (f32[2,6,1,128]{3,2,1,0:T(1,128)S(1)}, f32[2,6,1,128]{3,2,1,0:T(1,128)S(1)}, u32[]{:S(2)}, u32[]{:S(2)}) collective-permute-start(f32[2,6,1,128]{3,2,1,0:T(1,128)S(1)} %get-tuple-element.127), channel_id=1, source_target_pairs={{0,4},{4,8},{8,12},{12,0},{1,5},{5,9},{9,13},{13,1},{2,6},{6,10},{... | collective-permute-start | bytes 18440 | tf_op jit(solution)/shard_map/ppermute | solution.py:16
  247.0 6.4 %collective-permute-start.33 = (f32[2,6,1,128]{3,2,1,0:T(1,128)S(1)}, f32[2,6,1,128]{3,2,1,0:T(1,128)S(1)}, u32[]{:S(2)}, u32[]{:S(2)}) collective-permute-start(f32[2,6,1,128]{3,2,1,0:T(1,128)S(1)} %get-tuple-element.128), channel_id=1, source_target_pairs={{4,0},{8,4},{12,8},{0,12},{5,1},{9,5},{13,9},{1,13},{6,2},{10,6},{... | collective-permute-start | bytes 18440 | tf_op jit(solution)/shard_map/ppermute | solution.py:19
  253.6 7.4 %collective-permute-start.35 = (f32[2,6,10,1]{3,2,1,0:T(8,128)S(1)}, f32[2,6,10,1]{3,2,1,0:T(8,128)S(1)}, u32[]{:S(2)}, u32[]{:S(2)}) collective-permute-start(f32[2,6,10,1]{3,2,1,0:T(8,128)S(1)} %get-tuple-element.113), channel_id=1, source_target_pairs={{0,1},{1,2},{2,3},{3,0},{4,5},{5,6},{6,7},{7,4},{8,9},{9,10},{10,1... | collective-permute-start | bytes 1448 | tf_op jit(solution)/shard_map/ppermute | solution.py:16
  255.5 7.3 %collective-permute-start.34 = (f32[2,6,10,1]{3,2,1,0:T(8,128)S(1)}, f32[2,6,10,1]{3,2,1,0:T(8,128)S(1)}, u32[]{:S(2)}, u32[]{:S(2)}) collective-permute-start(f32[2,6,10,1]{3,2,1,0:T(8,128)S(1)} %get-tuple-element.114), channel_id=1, source_target_pairs={{1,0},{2,1},{3,2},{0,3},{5,4},{6,5},{7,6},{4,7},{9,8},{10,9},{11,1... | collective-permute-start | bytes 1448 | tf_op jit(solution)/shard_map/ppermute | solution.py:19
  272.9 8.7 %collective-permute-start.36 = (f32[2,1,8,128]{3,2,1,0:T(8,128)S(1)}, f32[2,1,8,128]{3,2,1,0:T(8,128)S(1)}, u32[]{:S(2)}, u32[]{:S(2)}) collective-permute-start(f32[2,1,8,128]{3,2,1,0:T(8,128)S(1)} %get-tuple-element.135), channel_id=1, source_target_pairs={{0,16},{16,32},{32,48},{48,64},{64,80},{80,96},{96,112},{112,128},... | collective-permute-start | bytes 24584 | tf_op jit(solution)/shard_map/ppermute | solution.py:16
  274.9 7.8 %collective-permute-start.37 = (f32[2,1,8,128]{3,2,1,0:T(8,128)S(1)}, f32[2,1,8,128]{3,2,1,0:T(8,128)S(1)}, u32[]{:S(2)}, u32[]{:S(2)}) collective-permute-start(f32[2,1,8,128]{3,2,1,0:T(8,128)S(1)} %get-tuple-element.136), channel_id=1, source_target_pairs={{16,0},{32,16},{48,32},{64,48},{80,64},{96,80},{112,96},{128,112},... | collective-permute-start | bytes 24584 | tf_op jit(solution)/shard_map/ppermute | solution.py:19
  282.7 8.3 %collective-permute-start.38 = (f32[2,6,1,128]{3,2,1,0:T(1,128)S(1)}, f32[2,6,1,128]{3,2,1,0:T(1,128)S(1)}, u32[]{:S(2)}, u32[]{:S(2)}) collective-permute-start(f32[2,6,1,128]{3,2,1,0:T(1,128)S(1)} %get-tuple-element.123), channel_id=1, source_target_pairs={{0,4},{4,8},{8,12},{12,0},{1,5},{5,9},{9,13},{13,1},{2,6},{6,10},{... | collective-permute-start | bytes 18440 | tf_op jit(solution)/shard_map/ppermute | solution.py:16
  286.1 5.5 %collective-permute-start.39 = (f32[2,6,1,128]{3,2,1,0:T(1,128)S(1)}, f32[2,6,1,128]{3,2,1,0:T(1,128)S(1)}, u32[]{:S(2)}, u32[]{:S(2)}) collective-permute-start(f32[2,6,1,128]{3,2,1,0:T(1,128)S(1)} %get-tuple-element.124), channel_id=1, source_target_pairs={{4,0},{8,4},{12,8},{0,12},{5,1},{9,5},{13,9},{1,13},{6,2},{10,6},{... | collective-permute-start | bytes 18440 | tf_op jit(solution)/shard_map/ppermute | solution.py:19
  291.8 7.4 %collective-permute-start.41 = (f32[2,6,10,1]{3,2,1,0:T(8,128)S(1)}, f32[2,6,10,1]{3,2,1,0:T(8,128)S(1)}, u32[]{:S(2)}, u32[]{:S(2)}) collective-permute-start(f32[2,6,10,1]{3,2,1,0:T(8,128)S(1)} %get-tuple-element.111), channel_id=1, source_target_pairs={{0,1},{1,2},{2,3},{3,0},{4,5},{5,6},{6,7},{7,4},{8,9},{9,10},{10,1... | collective-permute-start | bytes 1448 | tf_op jit(solution)/shard_map/ppermute | solution.py:16
  293.7 7.3 %collective-permute-start.40 = (f32[2,6,10,1]{3,2,1,0:T(8,128)S(1)}, f32[2,6,10,1]{3,2,1,0:T(8,128)S(1)}, u32[]{:S(2)}, u32[]{:S(2)}) collective-permute-start(f32[2,6,10,1]{3,2,1,0:T(8,128)S(1)} %get-tuple-element.112), channel_id=1, source_target_pairs={{1,0},{2,1},{3,2},{0,3},{5,4},{6,5},{7,6},{4,7},{9,8},{10,9},{11,1... | collective-permute-start | bytes 1448 | tf_op jit(solution)/shard_map/ppermute | solution.py:19
  308.5 8.7 %collective-permute-start.42 = (f32[2,1,8,128]{3,2,1,0:T(8,128)S(1)}, f32[2,1,8,128]{3,2,1,0:T(8,128)S(1)}, u32[]{:S(2)}, u32[]{:S(2)}) collective-permute-start(f32[2,1,8,128]{3,2,1,0:T(8,128)S(1)} %get-tuple-element.133), channel_id=1, source_target_pairs={{0,16},{16,32},{32,48},{48,64},{64,80},{80,96},{96,112},{112,128},... | collective-permute-start | bytes 24584 | tf_op jit(solution)/shard_map/ppermute | solution.py:16
  310.4 7.8 %collective-permute-start.43 = (f32[2,1,8,128]{3,2,1,0:T(8,128)S(1)}, f32[2,1,8,128]{3,2,1,0:T(8,128)S(1)}, u32[]{:S(2)}, u32[]{:S(2)}) collective-permute-start(f32[2,1,8,128]{3,2,1,0:T(8,128)S(1)} %get-tuple-element.134), channel_id=1, source_target_pairs={{16,0},{32,16},{48,32},{64,48},{80,64},{96,80},{112,96},{128,112},... | collective-permute-start | bytes 24584 | tf_op jit(solution)/shard_map/ppermute | solution.py:19
  318.2 8.0 %collective-permute-start.44 = (f32[2,6,1,128]{3,2,1,0:T(1,128)S(1)}, f32[2,6,1,128]{3,2,1,0:T(1,128)S(1)}, u32[]{:S(2)}, u32[]{:S(2)}) collective-permute-start(f32[2,6,1,128]{3,2,1,0:T(1,128)S(1)} %get-tuple-element.119), channel_id=1, source_target_pairs={{0,4},{4,8},{8,12},{12,0},{1,5},{5,9},{9,13},{13,1},{2,6},{6,10},{... | collective-permute-start | bytes 18440 | tf_op jit(solution)/shard_map/ppermute | solution.py:16
  322.1 5.5 %collective-permute-start.45 = (f32[2,6,1,128]{3,2,1,0:T(1,128)S(1)}, f32[2,6,1,128]{3,2,1,0:T(1,128)S(1)}, u32[]{:S(2)}, u32[]{:S(2)}) collective-permute-start(f32[2,6,1,128]{3,2,1,0:T(1,128)S(1)} %get-tuple-element.120), channel_id=1, source_target_pairs={{4,0},{8,4},{12,8},{0,12},{5,1},{9,5},{13,9},{1,13},{6,2},{10,6},{... | collective-permute-start | bytes 18440 | tf_op jit(solution)/shard_map/ppermute | solution.py:19
  327.8 7.4 %collective-permute-start.47 = (f32[2,6,10,1]{3,2,1,0:T(8,128)S(1)}, f32[2,6,10,1]{3,2,1,0:T(8,128)S(1)}, u32[]{:S(2)}, u32[]{:S(2)}) collective-permute-start(f32[2,6,10,1]{3,2,1,0:T(8,128)S(1)} %get-tuple-element.109), channel_id=1, source_target_pairs={{0,1},{1,2},{2,3},{3,0},{4,5},{5,6},{6,7},{7,4},{8,9},{9,10},{10,1... | collective-permute-start | bytes 1448 | tf_op jit(solution)/shard_map/ppermute | solution.py:16
  329.7 7.3 %collective-permute-start.46 = (f32[2,6,10,1]{3,2,1,0:T(8,128)S(1)}, f32[2,6,10,1]{3,2,1,0:T(8,128)S(1)}, u32[]{:S(2)}, u32[]{:S(2)}) collective-permute-start(f32[2,6,10,1]{3,2,1,0:T(8,128)S(1)} %get-tuple-element.110), channel_id=1, source_target_pairs={{1,0},{2,1},{3,2},{0,3},{5,4},{6,5},{7,6},{4,7},{9,8},{10,9},{11,1... | collective-permute-start | bytes 1448 | tf_op jit(solution)/shard_map/ppermute | solution.py:19
  (111 other events, 1595.5 us)
